TPU v7x, 128 devices: a whole 4x4x4 slice. The times are simulated.
128 devices in a mesh: heads: 4 (over y), tower: 2 (over z_lo), blk: 16 (over z_hi, x, core).
Axes of the slice: x: 4, y: 4, z: 4 (z_hi: 2, z_lo: 2; z = z_hi * 2 + z_lo), core: 2. Of those that a mesh axis runs over, the one named last changes fastest.
Arguments:
- query_input: bfloat16 [6144, 3584], P(('tower', 'blk'), 'heads'), may hold values from -6 to 6
- key_input: bfloat16 [6144, 512], P(('tower', 'blk'), 'heads'), may hold values from -6 to 6
- value_input: bfloat16 [6144, 512], P(('tower', 'blk'), 'heads'), may hold values from -6 to 6
- output_grad: bfloat16 [6144, 3584], P(('tower', 'blk'), 'heads'), may hold values from -6 to 6
- query_gain: float32 [2, 128], P('tower'), may hold values from 0.6 to 5
- key_gain: float32 [2, 128], P('tower'), may hold values from 0.6 to 5
- stripe_order: int32 [96], replicated, may hold values from 0 to 95, each once
- frame_index: int32 [48], replicated, may hold values from 0 to 11, never falling along the last dimension, each value on 1 to 8 neighbouring positions
- cross_blocks: int32 [96, 96], replicated, may hold values 0 or 1
Outputs:
- query_grad: bfloat16 [6144, 3584], P(('tower', 'blk'), 'heads')
- key_grad: bfloat16 [6144, 512], P(('tower', 'blk'), 'heads')
- value_grad: bfloat16 [6144, 512], P(('tower', 'blk'), 'heads')
- gain_grads: float32 [2, 2, 128], P(None, 'tower')
All inputs are finite; a program needn't handle non-finite values.
Results may differ from a plain program's by a relative error of at most 0.02.
The roundings to bfloat16 on the way count: a program that leaves them out, or rounds other values in their place, can miss the bound.
Values may be sent and summed in bfloat16 or wider, within the bound.
A program may use at most 64 MiB of HBM per device.

v0:
```python
import math

import jax
import jax.numpy as jnp
from jax import lax
from jax.sharding import Mesh
from jax.sharding import PartitionSpec as P

SEGMENT = 64
BLK = ("blk_0", "blk_1", "blk_2")
TOWER_BLK = ("tower", "blk_0", "blk_1", "blk_2")
HEADS_BLK = ("heads", "blk_0", "blk_1", "blk_2")


EPSILON = 1e-06
NEGATIVE = -1e30
block_rows = 384


def sent_to_all(array, axis):
    size = lax.axis_size(axis)
    return lax.all_to_all(
        jnp.broadcast_to(array[None], (size, *array.shape)), axis, 0, 0, tiled=True
    )


def laid_out(parts, dim):
    parts = jnp.moveaxis(parts, 0, dim)
    lengths = parts.shape
    return parts.reshape(*lengths[:dim], lengths[dim] * lengths[dim + 1], *lengths[dim + 2 :])


def gather_axes(array, axes, dim):
    far, near = axes
    parts = sent_to_all(sent_to_all(array, far), near)
    return laid_out(parts.swapaxes(0, 1).reshape(-1, *array.shape), dim)


def sent_together(arrays, axis, dim, along):
    both = jnp.concatenate(arrays, axis=along)
    result, at, gathered = (gather_axes(both, axis, dim), 0, [])
    for a in arrays:
        gathered.append(lax.slice_in_dim(result, at, at + a.shape[along], axis=along))
        at += a.shape[along]
    return tuple(gathered)


def in_blocks(array, dim, size):
    lengths = array.shape
    parts = array.reshape(*lengths[:dim], size, lengths[dim] // size, *lengths[dim + 1 :])
    return jnp.moveaxis(parts, dim, 0)


def sum_at_owner(array, axis, dim):
    parts = in_blocks(array, dim, lax.axis_size(axis))
    arrived = lax.all_to_all(parts, axis, split_axis=0, concat_axis=0, tiled=True)
    return arrived.astype(jnp.float32).sum(axis=0)


def summed_rows(array, axes, dim):
    far, near = axes
    parts = in_blocks(array, dim, lax.axis_size(far))
    nearer = sum_at_owner(parts, near, dim + 1)
    arrived = lax.all_to_all(
        nearer.astype(jnp.bfloat16), far, split_axis=0, concat_axis=0, tiled=True
    )
    return arrived.astype(jnp.float32).sum(axis=0)


def taken_together(array, axis):
    return sent_to_all(array, axis).sum(axis=0)


def together(arrays, axis):
    line, at, gathered = (jnp.concatenate([a.reshape(-1) for a in arrays]), 0, [])
    subtotal = taken_together(line, axis)
    for a in arrays:
        gathered.append(subtotal[at : at + a.size].reshape(a.shape))
        at += a.size
    return tuple(gathered)


def row_order(stripe_order, first, count, seg_len):
    slots = lax.dynamic_slice_in_dim(stripe_order, first, count)
    return (slots[:, None] * seg_len + jnp.arange(seg_len, dtype=jnp.int32)[None, :]).reshape(-1)


def allowed_pairs(
    query_first, query_segs, key_first, key_segs, stripe_order, frame_all, cross_blocks, seg_len
):
    half_segs = stripe_order.shape[0] // 2
    query_first = jnp.asarray(query_first, jnp.int32)
    key_first = jnp.asarray(key_first, jnp.int32)
    query_place = row_order(stripe_order, query_first, query_segs, seg_len).reshape(
        query_segs, seg_len, 1, 1
    )
    key_place = row_order(stripe_order, key_first, key_segs, seg_len).reshape(
        1, 1, key_segs, seg_len
    )
    query_frame = lax.dynamic_slice_in_dim(frame_all, query_first, query_segs)
    key_frame = lax.dynamic_slice_in_dim(frame_all, key_first, key_segs)
    same_frame = (query_frame[:, None] == key_frame[None, :]) & (query_frame[:, None] >= 0)
    query_image = query_first + jnp.arange(query_segs, dtype=jnp.int32) >= half_segs
    key_image = key_first + jnp.arange(key_segs, dtype=jnp.int32) >= half_segs
    opened = lax.dynamic_slice(cross_blocks, (query_first, key_first), (query_segs, key_segs)) == 1
    segment_open = (query_image[:, None] == key_image[None, :]) | opened
    allowed = ((key_place <= query_place) | same_frame[:, None, :, None]) & segment_open[
        :, None, :, None
    ]
    return allowed.reshape(query_segs * seg_len, key_segs * seg_len)


def unit_rows(raw, gain):
    values = raw.astype(jnp.float32)
    inverse = lax.rsqrt(jnp.mean(values * values, axis=-1, keepdims=True) + EPSILON)
    unit = values * inverse
    return (unit, inverse, (unit * gain).astype(jnp.bfloat16))


def unit_grad(grad, unit, inverse, gain):
    scaled = grad * gain
    return inverse * (scaled - unit * jnp.mean(scaled * unit, axis=-1, keepdims=True))


def shards(
    query_input,
    key_input,
    value_input,
    output_grad,
    query_gain,
    key_gain,
    stripe_order,
    frame_index,
    cross_blocks,
):
    rows = query_input.shape[0]
    head_dim = query_gain.shape[-1]
    groups = key_input.shape[1] // head_dim
    per_group = query_input.shape[1] // (groups * head_dim)
    scale = 1.0 / math.sqrt(head_dim)
    half_segs = stripe_order.shape[0] // 2
    frame_all = jnp.concatenate([jnp.full((half_segs,), -1, jnp.int32), frame_index])
    place = lax.axis_index("tower") * lax.axis_size(BLK) + lax.axis_index(BLK)
    query_first = place * rows // SEGMENT
    query_segs = rows // SEGMENT
    q_unit, q_inverse, q_normed = unit_rows(
        query_input.reshape(rows, groups, per_group, head_dim), query_gain[0]
    )
    k_unit, k_inverse, k_normed = unit_rows(key_input.reshape(rows, groups, head_dim), key_gain[0])
    key_flat = k_normed.reshape(rows, groups * head_dim)
    douts = output_grad.reshape(rows, groups, per_group, head_dim)
    whole_keys, whole_values = sent_together(
        (key_flat, value_input), (("tower", "blk_0", "blk_1"), "blk_2"), 0, 1
    )

    def logits_of(keys, allowed):
        products = jnp.einsum("rghd,kgd->rghk", q_normed, keys, preferred_element_type=jnp.float32)
        return jnp.where(allowed, products * scale, NEGATIVE)

    def over_keys(key_piece, value_piece, key_start, step, init):
        count = key_piece.shape[0]
        size = math.gcd(count, block_rows)

        def one_block(index, state):
            offset = index * size
            keys = lax.dynamic_slice_in_dim(key_piece, offset, size).reshape(size, groups, head_dim)
            values = lax.dynamic_slice_in_dim(value_piece, offset, size).reshape(
                size, groups, head_dim
            )
            first = (key_start + offset) // SEGMENT
            allowed = allowed_pairs(
                query_first,
                query_segs,
                first,
                size // SEGMENT,
                stripe_order,
                frame_all,
                cross_blocks,
                SEGMENT,
            )[:, None, None, :]
            return step(state, keys, values, allowed, offset)

        return lax.fori_loop(0, count // size, one_block, init)

    def stats_step(state, keys, values, allowed, offset):
        top, total, summed = state
        logits = logits_of(keys, allowed)
        new_top = jnp.maximum(top, jnp.max(logits, axis=-1))
        factor = jnp.exp(top - new_top)
        weights = jnp.where(allowed, jnp.exp(logits - new_top[..., None]), 0.0)
        total = total * factor + jnp.sum(weights, axis=-1)
        summed = summed * factor[..., None] + jnp.einsum(
            "rghk,kgd->rghd",
            weights.astype(jnp.bfloat16),
            values,
            preferred_element_type=jnp.float32,
        )
        return (new_top, total, summed)

    start_stats = (
        jnp.full((rows, groups, per_group), NEGATIVE, jnp.float32),
        jnp.zeros((rows, groups, per_group), jnp.float32),
        jnp.zeros((rows, groups, per_group, head_dim), jnp.float32),
    )
    top, total, summed = over_keys(whole_keys, whole_values, 0, stats_step, start_stats)
    output = lax.optimization_barrier((summed / total[..., None]).astype(jnp.bfloat16)).astype(
        jnp.float32
    )
    lse = top + jnp.log(total)
    delta = jnp.sum(douts.astype(jnp.float32) * output, axis=-1)

    def slopes_of(keys, values, allowed):
        weights = jnp.exp(logits_of(keys, allowed) - lse[..., None])
        pushes = jnp.einsum("rghd,kgd->rghk", douts, values, preferred_element_type=jnp.float32)
        return (weights, (weights * (pushes - delta[..., None])).astype(jnp.bfloat16))

    zero_query = jnp.zeros((rows, groups, per_group, head_dim), jnp.float32)

    def merged_step(state, keys, values, allowed, offset):
        grad_q, grad_kv = state
        weights, slopes = slopes_of(keys, values, allowed)
        size = keys.shape[0]
        grad_q = (
            grad_q
            + jnp.einsum("rghk,kgd->rghd", slopes, keys, preferred_element_type=jnp.float32) * scale
        )
        grad_key = (
            jnp.einsum("rghk,rghd->kgd", slopes, q_normed, preferred_element_type=jnp.float32)
            * scale
        )
        grad_val = jnp.einsum(
            "rghk,rghd->kgd",
            weights.astype(jnp.bfloat16),
            douts,
            preferred_element_type=jnp.float32,
        )
        block = jnp.concatenate([grad_key.reshape(size, -1), grad_val.reshape(size, -1)], axis=1)
        return (grad_q, lax.dynamic_update_slice_in_dim(grad_kv, block, offset, 0))

    empty_kv = jnp.zeros((whole_keys.shape[0], 2 * groups * head_dim), jnp.float32)
    grad_qn, key_full = over_keys(whole_keys, whole_values, 0, merged_step, (zero_query, empty_kv))
    query_grad = unit_grad(grad_qn, q_unit, q_inverse, query_gain[0])
    query_part = jnp.sum(grad_qn * q_unit, axis=(0, 1, 2))
    key_mine = summed_rows(key_full.astype(jnp.bfloat16), (("tower", "blk_0", "blk_1"), "blk_2"), 0)
    grad_kn = key_mine[:, : groups * head_dim].reshape(rows, groups, head_dim)
    grad_value = key_mine[:, groups * head_dim :]
    key_grad = unit_grad(grad_kn, k_unit, k_inverse, key_gain[0])
    key_part = jnp.sum(grad_kn * k_unit, axis=(0, 1))
    query_total, key_total = together((query_part, key_part), HEADS_BLK)
    gain_grads = jnp.stack([query_total, key_total])[:, None, :]
    return (
        query_grad.reshape(rows, -1).astype(jnp.bfloat16),
        key_grad.reshape(rows, -1).astype(jnp.bfloat16),
        grad_value.astype(jnp.bfloat16),
        gain_grads,
    )


def solution(mesh):
    split = Mesh(
        mesh.devices.reshape(mesh.shape["heads"], mesh.shape["tower"], 2, 4, 2),
        ("heads", "tower", "blk_0", "blk_1", "blk_2"),
    )
    in_specs = (
        P(TOWER_BLK, "heads"),
        P(TOWER_BLK, "heads"),
        P(TOWER_BLK, "heads"),
        P(TOWER_BLK, "heads"),
        P("tower", None),
        P("tower", None),
        P(),
        P(),
        P(),
    )
    out_specs = (
        P(TOWER_BLK, "heads"),
        P(TOWER_BLK, "heads"),
        P(TOWER_BLK, "heads"),
        P(None, "tower", None),
    )
    return jax.shard_map(
        shards, mesh=split, in_specs=in_specs, out_specs=out_specs, check_vma=False
    )
```

profile of v0, /device:TPU:1, one launch (start us, length us, event | category | flops | bytes accessed | tf_op | source)
XLA Modules:
  0.0 370.5 jit_solution(14062401875342729338)
XLA Ops:
  4.6 8.6 %all-to-all-start = ((bf16[16,192,256]{2,1,0:T(8,128)(2,1)}), bf16[16,192,256]{2,1,0:T(8,128)(2,1)}, u32[]{:S(2)}, u32[]{:S(2)}) async-start(bf16[16,192,256]{2,1,0:T(8,128)(2,1)} %broadcast_in_dim.176), calls=%async_computation | async-start | bytes 3145728 | tf_op jit(solution)/shard_map/all_to_all | solution.py:22
  15.1 21.3 %all-to-all-done = bf16[16,192,256]{2,1,0:T(8,128)(2,1)} async-done(((bf16[16,192,256]{2,1,0:T(8,128)(2,1)}), bf16[16,192,256]{2,1,0:T(8,128)(2,1)}, u32[]{:S(2)}, u32[]{:S(2)}) %all-to-all-start) | async-done | bytes 1572896 | tf_op jit(solution)/shard_map/all_to_all | solution.py:22
  36.3 1.8 broadcast_in_dim.177
  38.1 8.3 %all_to_all.26 = bf16[2,16,192,256]{3,2,1,0:T(8,128)(2,1)S(1)} all-to-all(bf16[2,16,192,256]{3,2,1,0:T(8,128)(2,1)S(1)} %broadcast_in_dim.177), channel_id=1, replica_groups=mesh['heads'=4,'tower'=2,'blk_0'=2,'blk_1'=4,'blk_2'=2] {'blk_2'}, dimensions={0} | all-to-all | bytes 6291456 | tf_op jit(solution)/shard_map/all_to_all | solution.py:22
  46.7 1.9 fusion.60
  48.6 120.6 %while.38 = (s32[]{:T(128)}, f32[192,1,7]{0,2,1:T(8,128)S(1)}, f32[192,1,7]{0,2,1:T(8,128)S(1)}, f32[192,1,7,128]{3,0,2,1:T(8,128)}, s32[96]{0:T(128)S(1)}, /*in...) while((s32[]{:T(128)}, f32[192,1,7]{0,2,1:T(8,128)S(1)}, ...), condition=%wide.region_5.6_spmd.clone, body=%wide.region_2.5_spmd.clone.sunk | while | flops 271696448 | bytes 14605186 | solution.py:183
  50.9 1.6 fusion.88
  53.5 1.8 fusion.91
  58.5 1.6 fusion.88
  61.0 1.8 fusion.91
  66.0 1.6 fusion.88
  68.6 1.8 fusion.91
  73.6 1.6 fusion.88
  76.1 1.8 fusion.91
  81.1 1.6 fusion.88
  83.6 1.8 fusion.91
  88.6 1.6 fusion.88
  91.2 1.8 fusion.91
  96.2 1.6 fusion.88
  98.7 1.8 fusion.91
  103.7 1.6 fusion.88
  106.2 1.8 fusion.91
  111.2 1.6 fusion.88
  113.8 1.8 fusion.91
  118.8 1.6 fusion.88
  121.3 1.8 fusion.91
  126.3 1.6 fusion.88
  128.9 1.8 fusion.91
  133.9 1.6 fusion.88
  136.4 1.8 fusion.91
  141.4 1.6 fusion.88
  143.9 1.8 fusion.91
  148.9 1.6 fusion.88
  151.5 1.8 fusion.91
  156.5 1.6 fusion.88
  159.0 1.8 fusion.91
  164.0 1.6 fusion.88
  166.5 1.8 fusion.91
  169.3 1.6 fusion.48
  171.3 1.9 broadcast_in_dim.175.clone
  173.2 136.5 %while.39 = (s32[]{:T(128)}, f32[192,1,7,128]{3,0,2,1:T(8,128)S(1)}, bf16[6144,256]{1,0:T(8,128)(2,1)}, bf16[6144,128]{1,0:T(8,128)(2,1)}, s32[96]{0:T(128)S(1)}...) while((s32[]{:T(128)}, ...), condition=%wide.region_8.9_spmd.clone, body=%wide.region_7.8_spmd.clone.sunk | while | flops 665445056 | bytes 14480736 | solution.py:183
  175.5 1.6 fusion.103
  184.1 1.6 fusion.103
  192.6 1.6 fusion.103
  201.1 1.6 fusion.103
  209.6 1.6 fusion.103
  218.2 1.6 fusion.103
  226.7 1.6 fusion.103
  235.2 1.6 fusion.103
  243.7 1.6 fusion.103
  252.3 1.6 fusion.103
  260.8 1.6 fusion.103
  269.4 1.6 fusion.103
  277.9 1.6 fusion.103
  286.4 1.6 fusion.103
  295.0 1.6 fusion.103
  303.5 1.6 fusion.103
  309.7 2.2 copy.68
  311.9 7.3 %all_to_all.27 = bf16[2,16,192,256]{3,2,1,0:T(8,128)(2,1)} all-to-all(bf16[2,16,192,256]{3,2,1,0:T(8,128)(2,1)S(1)} %copy.68), channel_id=1, replica_groups=mesh['heads'=4,'tower'=2,'blk_0'=2,'blk_1'=4,'blk_2'=2] {'blk_2'}, dimensions={0} | all-to-all | bytes 6291456 | tf_op jit(solution)/shard_map/all_to_all | solution.py:56
  319.2 4.1 %reduce_sum.113 = bf16[16,192,256]{2,1,0:T(8,128)(2,1)} reduce(bf16[2,16,192,256]{3,2,1,0:T(8,128)(2,1)} %all_to_all.27, bf16[]{:T(256)} %constant.326.clone.1), dimensions={0}, to_apply=%region_10.11 | reduce | flops 786432 | bytes 4718594 | tf_op jit(solution)/shard_map/reduce_sum | solution.py:57
  323.3 3.7 %all-to-all-start.3 = ((bf16[16,192,256]{2,1,0:T(8,128)(2,1)}), bf16[16,192,256]{2,1,0:T(8,128)(2,1)S(1)}, u32[]{:S(2)}, u32[]{:S(2)}) async-start(bf16[16,192,256]{2,1,0:T(8,128)(2,1)} %reduce_sum.113), calls=%async_computation.3 | async-start | bytes 3145728 | tf_op jit(solution)/shard_map/all_to_all | solution.py:64
  329.2 23.7 %all-to-all-done.3 = bf16[16,192,256]{2,1,0:T(8,128)(2,1)S(1)} async-done(((bf16[16,192,256]{2,1,0:T(8,128)(2,1)}), bf16[16,192,256]{2,1,0:T(8,128)(2,1)S(1)}, u32[]{:S(2)}, u32[]{:S(2)}) %all-to-all-start.3) | async-done | bytes 1572896 | tf_op jit(solution)/shard_map/all_to_all | solution.py:64
  354.0 6.2 %all-to-all-start.4 = ((f32[64,1,256]{2,1,0:T(1,128)}), f32[64,1,256]{2,1,0:T(1,128)S(1)}, u32[]{:S(2)}, u32[]{:S(2)}) async-start(f32[64,1,256]{2,1,0:T(1,128)} %broadcast_in_dim.180), calls=%async_computation.4 | async-start | bytes 131072 | tf_op jit(solution)/shard_map/all_to_all | solution.py:22
  361.5 8.2 %all-to-all-done.4 = f32[64,1,256]{2,1,0:T(1,128)S(1)} async-done(((f32[64,1,256]{2,1,0:T(1,128)}), f32[64,1,256]{2,1,0:T(1,128)S(1)}, u32[]{:S(2)}, u32[]{:S(2)}) %all-to-all-start.4) | async-done | bytes 65568 | tf_op jit(solution)/shard_map/all_to_all | solution.py:22
  (900 shorter events, 186.6 us)
Async XLA Ops:
  3.3 10.0 %copy-start.7 = (s32[48]{0:T(128)S(1)}, s32[48]{0:T(128)}, u32[]{:S(2)}) copy-start(s32[48]{0:T(128)} %param.20) | copy-start | bytes 580
  3.3 10.1 %copy-start.3 = (bf16[192,896]{1,0:T(8,128)(2,1)S(1)}, bf16[192,896]{1,0:T(8,128)(2,1)}, u32[]{:S(2)}) copy-start(bf16[192,896]{1,0:T(8,128)(2,1)} %param.16) | copy-start | bytes 1032196
  4.6 9.2 %copy-start.4 = (bf16[192,896]{1,0:T(8,128)(2,1)S(1)}, bf16[192,896]{1,0:T(8,128)(2,1)}, u32[]{:S(2)}) copy-start(bf16[192,896]{1,0:T(8,128)(2,1)} %param.13) | copy-start | bytes 1032196
  4.6 31.7 %all-to-all-start = ((bf16[16,192,256]{2,1,0:T(8,128)(2,1)}), bf16[16,192,256]{2,1,0:T(8,128)(2,1)}, u32[]{:S(2)}, u32[]{:S(2)}) async-start(bf16[16,192,256]{2,1,0:T(8,128)(2,1)} %broadcast_in_dim.176), calls=%async_computation | async-start | bytes 3145728 | tf_op jit(solution)/shard_map/all_to_all | solution.py:22
  13.2 1.4 copy-start.5
  13.8 1.1 copy-start.8
  50.9 2.5 copy-start.1
  55.3 0.8 copy-start.2
  58.5 2.6 copy-start.1
  62.8 0.8 copy-start.2
  66.0 2.5 copy-start.1
  70.4 0.8 copy-start.2
  73.5 2.5 copy-start.1
  77.9 0.8 copy-start.2
  81.1 2.6 copy-start.1
  85.4 0.8 copy-start.2
  88.6 2.5 copy-start.1
  93.0 0.8 copy-start.2
  96.2 2.5 copy-start.1
  100.5 0.8 copy-start.2
  103.7 2.6 copy-start.1
  108.0 0.8 copy-start.2
  111.2 2.5 copy-start.1
  115.6 0.8 copy-start.2
  118.8 2.5 copy-start.1
  123.1 0.8 copy-start.2
  126.3 2.6 copy-start.1
  130.7 0.8 copy-start.2
  133.8 2.5 copy-start.1
  138.2 0.8 copy-start.2
  141.4 2.5 copy-start.1
  145.7 0.8 copy-start.2
  148.9 2.6 copy-start.1
  153.3 0.8 copy-start.2
  156.5 2.5 copy-start.1
  160.8 0.8 copy-start.2
  164.0 2.5 copy-start.1
  168.3 0.8 copy-start.2
  323.3 29.6 %all-to-all-start.3 = ((bf16[16,192,256]{2,1,0:T(8,128)(2,1)}), bf16[16,192,256]{2,1,0:T(8,128)(2,1)S(1)}, u32[]{:S(2)}, u32[]{:S(2)}) async-start(bf16[16,192,256]{2,1,0:T(8,128)(2,1)} %reduce_sum.113), calls=%async_computation.3 | async-start | bytes 3145728 | tf_op jit(solution)/shard_map/all_to_all | solution.py:64
  327.8 25.3 %copy-start = (bf16[192,128]{1,0:T(8,128)(2,1)S(1)}, bf16[192,128]{1,0:T(8,128)(2,1)}, u32[]{:S(2)}) copy-start(bf16[192,128]{1,0:T(8,128)(2,1)} %param.14) | copy-start | bytes 147460
  327.8 25.3 %copy-start.6 = (f32[1,128]{1,0:T(1,128)S(1)}, f32[1,128]{1,0:T(1,128)}, u32[]{:S(2)}) copy-start(f32[1,128]{1,0:T(1,128)} %param.18) | copy-start | bytes 1540
  354.0 15.8 %all-to-all-start.4 = ((f32[64,1,256]{2,1,0:T(1,128)}), f32[64,1,256]{2,1,0:T(1,128)S(1)}, u32[]{:S(2)}, u32[]{:S(2)}) async-start(f32[64,1,256]{2,1,0:T(1,128)} %broadcast_in_dim.180), calls=%async_computation.4 | async-start | bytes 131072 | tf_op jit(solution)/shard_map/all_to_all | solution.py:22
where the time goes:
time: 375 us; the launch traced here: 370 us
  matrix products  139 us (37%)
  local copies, waits for them, and re-layouts  78 us (21%)
  other arithmetic  62.7 us (17%)
  waiting for transfers between devices  53.2 us (14%)
  starting transfers between devices  18.5 us (5%)
  blocking collectives  15.6 us (4%)
    dot_general x32, matrix products, logits_of(): jnp.einsum('rghd,kgd->rghk', q_normed, keys, preferred_element_type=jnp.f...  51.1 us
    all_to_all x2, waiting for transfers between devices, sent_to_all(): lax.all_to_all(jnp.broadcast_to(array[None], (size, *array.shape)), axis,...  29.5 us
    dot_general x16, matrix products, stats_step(): jnp.einsum('rghk,kgd->rghd', weights.astype(jnp.bfloat16), values, prefer...  28.6 us
    or x32, other arithmetic, allowed_pairs(): segment_open = (query_image[:, None] == key_image[None, :]) | opened  25.2 us
    all_to_all x1, waiting for transfers between devices, summed_rows(): lax.all_to_all(nearer.astype(jnp.bfloat16), far, split_axis=0, concat_axi...  23.7 us
    dot_general x16, matrix products, merged_step(): jnp.einsum('rghk,kgd->rghd', slopes, keys, preferred_element_type=jnp.flo...  23.7 us
    dot_general x16, matrix products, slopes_of(): jnp.einsum('rghd,kgd->rghk', douts, values, preferred_element_type=jnp.fl...  21.9 us
    all_to_all x2, starting transfers between devices, sent_to_all(): lax.all_to_all(jnp.broadcast_to(array[None], (size, *array.shape)), axis,...  14.8 us
  transfers between devices with their start and end apart: 3, of which 3 were waited for; matrix products, arithmetic and copies ran while one was open for 1% of the time, Pallas kernels for 0%

commit v1 on v0

v1 whole, which is shorter than its diff:
```python
import functools
import math

import jax
import jax.numpy as jnp
from jax import lax
from jax.experimental import pallas as pl
from jax.experimental.pallas import tpu as pltpu
from jax.sharding import Mesh
from jax.sharding import PartitionSpec as P

SEGMENT = 64
AXES = ("heads", "tower", "blk_0", "blk_1", "blk_2")
TOWER_BLK = ("tower", "blk_0", "blk_1", "blk_2")
EPSILON = 1e-06
NEGATIVE = -1e30
LOG2E = 1.4426950408889634
MESH = pl.DeviceIdType.MESH
VMEM = pltpu.VMEM
DMA = pltpu.SemaphoreType.DMA
F32, BF16, I32 = jnp.float32, jnp.bfloat16, jnp.int32


def dot(a, b, left, right):
    return lax.dot_general(a, b, (((left,), (right,)), ((), ())), preferred_element_type=F32)


def position():
    z = lax.axis_index("blk_0") * 2 + lax.axis_index("tower")
    return lax.axis_index("heads"), lax.axis_index("blk_1"), z, lax.axis_index("blk_2")


def device(y, x, z, core):
    return (y, lax.rem(z, 2), lax.div(z, 2), x, core)


def place_of(x, z, core):
    return lax.rem(z, 2) * 16 + lax.div(z, 2) * 8 + x * 2 + core


def shifted(x, z, core, first, second):
    nx = lax.rem(x + (1 - core) * first + core * second, 4)
    nz = lax.rem(z + core * first + (1 - core) * second, 4)
    return nx, nz


def remote(src, dst, send, recv, target):
    return pltpu.make_async_remote_copy(
        src_ref=src, dst_ref=dst, send_sem=send, recv_sem=recv, device_id=target, device_id_type=MESH
    )


def meet(targets):
    barrier = pltpu.get_barrier_semaphore()
    for target in targets:
        pl.semaphore_signal(barrier, inc=1, device_id=target, device_id_type=MESH)
    return lambda: pl.semaphore_wait(barrier, len(targets))


def gather_kernel(
    key_ref, value_ref, gain_ref, order_ref, frame_ref, cross_ref, all_ref, list_ref,
    mine, own_sem, send_a, recv_a, send_b, recv_b, send_s, recv_s,
):
    y, x, z, core = position()

    def target(first, second):
        nx, nz = shifted(x, z, core, first, second)
        return device(y, nx, nz, core)

    def chunk(first, second):
        nx, nz = shifted(x, z, core, first, second)
        return place_of(nx, nz, core)

    sibling = device(y, x, z, 1 - core)
    ring_a = (target(1, 0), target(3, 0))
    ring_b = (target(0, 1), target(0, 3))
    wait_all = meet((*ring_a, *ring_b, sibling))
    keys = key_ref[...].astype(F32)
    inverse = lax.rsqrt(jnp.mean(keys * keys, axis=-1, keepdims=True) + EPSILON)
    mine[0] = (keys * inverse * gain_ref[...]).astype(BF16)
    mine[1] = value_ref[...]
    me = place_of(x, z, core)
    own = pltpu.make_async_copy(mine, all_ref.at[me], own_sem)
    started = []

    def send(src, dst, send_sem, recv_sem, to):
        copy = remote(src, dst, send_sem, recv_sem, to)
        copy.start()
        started.append(copy)

    def arrived(dst, recv_sem):
        remote(dst, dst, send_s.at[0], recv_sem, sibling).wait_recv()

    def spread(first, src):
        at = all_ref.at[chunk(first, 0)]
        send(src, at, send_b.at[first, 0], recv_b.at[first, 1], ring_b[0])
        send(src, at, send_b.at[first, 1], recv_b.at[first, 0], ring_b[1])

    def share(first, second, src):
        n = first * 4 + second
        send(src, all_ref.at[chunk(first, second)], send_s.at[n], recv_s.at[n], sibling)

    wait_all()
    own.start()
    send(mine, all_ref.at[me], send_a.at[0], recv_a.at[1], ring_a[0])
    send(mine, all_ref.at[me], send_a.at[1], recv_a.at[0], ring_a[1])
    spread(0, mine)
    share(0, 0, mine)

    lane = lax.broadcasted_iota(I32, (1, 128), 1)
    down = lax.broadcasted_iota(I32, (128, 128), 0)
    across = lax.broadcasted_iota(I32, (128, 128), 1)
    order, frame = order_ref[...], frame_ref[...]
    below = (across < down).astype(F32)
    start_of = (lax.shift_right_logical(down * 171, 9) * 384 + (down - 3 * lax.shift_right_logical(down * 171, 9)) * 64)
    image = me >= 16
    list_ref[...] = jnp.zeros_like(list_ref)
    counts = jnp.where(lane == 3, jnp.where(image, 0, 1), 0)
    for b in range(3):
        block = me * 3 + b
        here = lane == block
        slot = jnp.sum(jnp.where(here, order, 0), axis=-1, keepdims=True)
        seen = jnp.sum(jnp.where(here, frame, 0), axis=-1, keepdims=True)
        same = (lane >= 48) == image
        near = (order <= slot) | ((frame == seen) & (seen >= 0))
        opened = same | (cross_ref[pl.ds(block, 1), :] == 1)
        others = (near & opened & (lane < 96) & (lane != block)).astype(F32)
        column = jnp.broadcast_to(others, (128, 128)).T
        at = dot(below, column, 1, 0).astype(I32) + 1
        chosen = (column > 0.5) & (at == across)
        listed = jnp.sum(jnp.where(chosen, start_of, 0), axis=0, keepdims=True)
        first_start = me * 384 + b * 64
        list_ref[b : b + 1, :] = jnp.where(lane == 0, first_start, listed)
        count = 1 + jnp.sum(others, axis=-1, keepdims=True).astype(I32)
        counts = jnp.where(lane == b, count, counts)
    list_ref[3:4, :] = counts

    def from_a(slot, first, half, to, forward_recv):
        at = all_ref.at[chunk(first, 0)]
        arrived(at, recv_a.at[slot])
        send(at.at[half], at.at[half], send_a.at[2 + half], recv_a.at[forward_recv], to)
        spread(first, at)
        share(first, 0, at)

    def from_b(first, slot, second, half, to):
        at = all_ref.at[chunk(first, second)]
        arrived(at, recv_b.at[first, slot])
        send(at.at[half], at.at[half], send_b.at[first, 2 + half], recv_b.at[first, 2 + half], to)
        share(first, second, at)

    def both_b(first):
        from_b(first, 0, 1, 0, ring_b[1])
        from_b(first, 1, 3, 1, ring_b[0])

    from_a(0, 1, 0, ring_a[1], 2)
    from_a(1, 3, 1, ring_a[0], 3)
    both_b(0)
    at = all_ref.at[chunk(2, 0)]
    arrived(at.at[0], recv_a.at[2])
    arrived(at.at[1], recv_a.at[3])
    spread(2, at)
    share(2, 0, at)
    both_b(1)
    both_b(3)
    both_b(2)
    for first in (0, 1, 3, 2):
        at = all_ref.at[chunk(first, 2)]
        arrived(at.at[0], recv_b.at[first, 2])
        arrived(at.at[1], recv_b.at[first, 3])
        share(first, 2, at)
    own.wait()
    for copy in started:
        copy.wait_send()
    for n in range(16):
        nx, nz = shifted(x, z, 1 - core, n // 4, n % 4)
        arrived(all_ref.at[place_of(nx, nz, 1 - core)], recv_s.at[n])


def gathered(key_input, value_input, key_gain, order, frame, cross):
    rows, dim = key_input.shape
    whole = pl.BlockSpec(memory_space=VMEM)
    return pl.pallas_call(
        gather_kernel,
        out_shape=(jax.ShapeDtypeStruct((32, 2, rows, dim), BF16), jax.ShapeDtypeStruct((8, 128), I32)),
        in_specs=[whole] * 6,
        out_specs=(pl.BlockSpec(memory_space=pl.ANY), whole),
        scratch_shapes=[
            VMEM((2, rows, dim), BF16), DMA, DMA((4,)), DMA((4,)), DMA((4, 4)), DMA((4, 4)), DMA((16,)), DMA((16,)),
        ],
        compiler_params=pltpu.CompilerParams(collective_id=0, has_side_effects=True),
        name="gather_keys",
    )(key_input, value_input, key_gain, order, frame, cross)


def attention_kernel(
    per_group, blocks, width, list_ref, query_ref, grad_ref, gain_ref, kv_ref,
    out_ref, gain_out, part_ref,
    qn, dop, s_ref, w_ref, m_ref, l_ref, o_ref, dq_ref, acc,
):
    dim = 128
    rows = SEGMENT * per_group
    per = width // SEGMENT
    log_scale = LOG2E / math.sqrt(dim)
    scale = 1.0 / math.sqrt(dim)
    places = kv_ref.shape[0] // 384
    is_text = list_ref[3, 3] == 1
    gain = gain_ref[...]

    def zero(i, _):
        acc[pl.ds(pl.multiple_of(i * 128, 128), 128), :] = jnp.zeros((128, dim), F32)
        return 0

    lax.fori_loop(0, places * 3, zero, 0)
    query_part = jnp.zeros((8, dim), F32)

    for b in range(blocks):
        count = list_ref[3, b]
        rest = lax.rem(count - 1, per)
        groups = lax.div(count - 1, per)
        for h in range(per_group):
            q = query_ref[b * SEGMENT : (b + 1) * SEGMENT, h * dim : (h + 1) * dim].astype(F32)
            inverse = lax.rsqrt(jnp.mean(q * q, axis=-1, keepdims=True) + EPSILON)
            qn[h * SEGMENT : (h + 1) * SEGMENT, :] = (q * inverse * gain).astype(BF16)
        m_ref[...] = jnp.full_like(m_ref, NEGATIVE)
        l_ref[...] = jnp.zeros_like(l_ref)
        o_ref[...] = jnp.zeros_like(o_ref)
        dq_ref[...] = jnp.zeros_like(dq_ref)

        def starts(g):
            out = []
            for j in range(per):
                if isinstance(g, int):
                    p = 0 if j == 0 else jnp.where(j <= rest, j, 0)
                else:
                    p = 1 + rest + (g - 1) * per + j
                out.append(pl.multiple_of(list_ref[b, p], SEGMENT))
            return out

        def tile(at, offset):
            return jnp.concatenate([kv_ref[pl.ds(s + offset, SEGMENT), :] for s in at], axis=0)

        def logits(g, at, masked):
            s = dot(qn[...], tile(at, 0), 1, 1)
            if masked:
                lane = lax.broadcasted_iota(I32, (rows, width), 1)
                row = lax.broadcasted_iota(I32, (rows, width), 0)
                limit = lax.rem(row, SEGMENT) + jnp.where(is_text, 0, SEGMENT)
                ok = (lane < (rest + 1) * SEGMENT) & ((lane >= SEGMENT) | (lane <= limit))
                s = jnp.where(ok, s, NEGATIVE)
            s_ref[g] = s
            top = m_ref[...]
            for t in range(width // 128):
                top = jnp.maximum(top, s[:, t * 128 : (t + 1) * 128])
            m_ref[...] = top

        def weights(g, at):
            top = m_ref[...]
            total = l_ref[...]
            parts = []
            for t in range(width // 128):
                w = jnp.exp2((s_ref[g, :, t * 128 : (t + 1) * 128] - top) * log_scale)
                total = total + w
                parts.append(w.astype(BF16))
            l_ref[...] = total
            w = jnp.concatenate(parts, axis=1)
            w_ref[g] = w
            o_ref[...] += dot(w, tile(at, 192), 1, 0)

        def slopes(g, at):
            keys = tile(at, 0)
            pushes = dot(dop[...], tile(at, 192), 1, 1)
            delta = m_ref[...]
            w = w_ref[g]
            parts = []
            for t in range(width // 128):
                sl = slice(t * 128, (t + 1) * 128)
                parts.append((w[:, sl].astype(F32) * (pushes[:, sl] - delta)).astype(BF16))
            ds = jnp.concatenate(parts, axis=1)
            dq_ref[...] += dot(ds, keys, 1, 0)
            dk = dot(ds, qn[...], 0, 0)
            dv = dot(w, dop[...], 0, 0)
            for j in range(per):
                sl = slice(j * SEGMENT, (j + 1) * SEGMENT)
                acc[pl.ds(at[j], SEGMENT), :] += dk[sl]
                acc[pl.ds(at[j] + 192, SEGMENT), :] += dv[sl]

        def over(step):
            def body(g, _):
                step(g, starts(g))
                return 0

            lax.fori_loop(1, groups + 1, body, 0)

        logits(0, starts(0), True)
        over(lambda g, at: logits(g, at, False))
        m_ref[...] = jnp.broadcast_to(jnp.max(m_ref[...], axis=-1, keepdims=True), m_ref.shape)
        weights(0, starts(0))
        over(weights)
        total = jnp.sum(l_ref[...], axis=-1, keepdims=True)
        over_total = 1.0 / total
        output = (o_ref[...] / total).astype(BF16).astype(F32)
        for h in range(per_group):
            sl = slice(h * SEGMENT, (h + 1) * SEGMENT)
            g = grad_ref[b * SEGMENT : (b + 1) * SEGMENT, h * dim : (h + 1) * dim].astype(F32)
            g = (g * over_total[sl]).astype(BF16)
            dop[sl, :] = g
            delta = jnp.sum(g.astype(F32) * output[sl], axis=-1, keepdims=True)
            m_ref[sl, :] = jnp.broadcast_to(delta, (SEGMENT, 128))
        slopes(0, starts(0))
        over(slopes)
        for h in range(per_group):
            sl = slice(h * SEGMENT, (h + 1) * SEGMENT)
            q = query_ref[b * SEGMENT : (b + 1) * SEGMENT, h * dim : (h + 1) * dim].astype(F32)
            inverse = lax.rsqrt(jnp.mean(q * q, axis=-1, keepdims=True) + EPSILON)
            unit = q * inverse
            grad = dq_ref[sl, :] * scale
            e = grad * gain
            dq = inverse * (e - unit * jnp.mean(e * unit, axis=-1, keepdims=True))
            out_ref[b * SEGMENT : (b + 1) * SEGMENT, h * dim : (h + 1) * dim] = dq.astype(BF16)
            query_part = query_part + jnp.sum((grad * unit).reshape(SEGMENT // 8, 8, dim), axis=0)

    def finish(i, part):
        at = pl.multiple_of(i * 384, 384)
        mine = acc[pl.ds(at, 384), :]
        part_ref[i, 0] = mine[:192].astype(BF16)
        part_ref[i, 1] = mine[192:].astype(BF16)
        terms = mine[:192] * kv_ref[pl.ds(at, 192), :].astype(F32)
        return part + jnp.sum(terms.reshape(24, 8, dim), axis=0)

    text = lax.fori_loop(0, places // 2, finish, jnp.zeros((8, dim), F32))
    image = lax.fori_loop(places // 2, places, finish, jnp.zeros((8, dim), F32))
    query_sum = jnp.sum(query_part, axis=0, keepdims=True)
    row = lax.broadcasted_iota(I32, (8, dim), 0)
    filled = jnp.where(row == jnp.where(is_text, 0, 1), query_sum, 0.0)
    filled = jnp.where(row == 2, jnp.sum(text, axis=0, keepdims=True), filled)
    gain_out[...] = jnp.where(row == 3, jnp.sum(image, axis=0, keepdims=True), filled)


def attention(lists, query_input, output_grad, query_gain, kv, width):
    rows, columns = query_input.shape
    per_group = columns // 128
    stacked = SEGMENT * per_group
    segments = kv.shape[0] * 3
    per = width // SEGMENT
    groups = (segments + per - 1) // per + 1
    flat = kv.shape[0] * 384
    whole = pl.BlockSpec(memory_space=VMEM)
    return pl.pallas_call(
        functools.partial(attention_kernel, per_group, rows // SEGMENT, width),
        out_shape=(
            jax.ShapeDtypeStruct((rows, columns), BF16),
            jax.ShapeDtypeStruct((8, 128), F32),
            jax.ShapeDtypeStruct(kv.shape, BF16),
        ),
        in_specs=[pl.BlockSpec(memory_space=pltpu.SMEM)] + [whole] * 4,
        out_specs=(whole,) * 3,
        scratch_shapes=[
            VMEM((stacked, 128), BF16), VMEM((stacked, 128), BF16),
            VMEM((groups, stacked, width), F32), VMEM((groups, stacked, width), BF16),
            VMEM((stacked, 128), F32), VMEM((stacked, 128), F32), VMEM((stacked, 128), F32), VMEM((stacked, 128), F32),
            VMEM((flat, 128), F32),
        ],
        compiler_params=pltpu.CompilerParams(vmem_limit_bytes=60 * 1024 * 1024),
        name="attention",
    )(lists, query_input, output_grad, query_gain, kv.reshape(flat, 128))


def reduce_kernel(
    part_ref, gain_part, key_ref, gain_ref, key_out, value_out, gain_out,
    sib, work, half_b, full_b, half_a, full_a, sums,
    send_s, recv_s, send_hb, recv_hb, send_fb, recv_fb, send_a, recv_a, send_g, recv_g,
):
    y, x, z, core = position()
    scale = 1.0 / math.sqrt(128)

    def target(first, second):
        nx, nz = shifted(x, z, core, first, second)
        return device(y, nx, nz, core)

    sibling = device(y, x, z, 1 - core)
    ring_a = (target(1, 0), target(3, 0))
    ring_b = (target(0, 1), target(0, 3))
    lines = (
        (y, 4, lambda n: device(n, x, z, core)),
        (core, 2, lambda n: device(y, x, z, n)),
        (x, 4, lambda n: device(y, n, z, core)),
        (z, 4, lambda n: device(y, x, n, core)),
    )
    peers = [sibling]
    for at, size, of in lines[:1] + lines[2:]:
        peers += [of(lax.rem(at + o, size)) for o in range(1, size)]
    meet(peers)()
    started = []

    def send(src, dst, send_sem, recv_sem, to):
        copy = remote(src, dst, send_sem, recv_sem, to)
        copy.start()
        started.append(copy)

    def arrived(dst, recv_sem):
        remote(dst, dst, send_s.at[0], recv_sem, sibling).wait_recv()

    def gain_send(stage, value):
        at, size, of = lines[stage]
        sums[stage, at] = value
        for o in range(1, size):
            send(sums.at[stage, at], sums.at[stage, at], send_g.at[stage, o], recv_g.at[stage, at], of(lax.rem(at + o, size)))

    def gain_sum(stage):
        at, size, of = lines[stage]
        for o in range(1, size):
            n = lax.rem(at + o, size)
            arrived(sums.at[stage, n], recv_g.at[stage, n])
        total = sums[stage, 0]
        for n in range(1, size):
            total = total + sums[stage, n]
        return total

    visit = [(first, second) for second in (2, 1, 3, 0) for first in (2, 1, 3, 0)]
    for first, second in visit:
        nx, nz = shifted(x, z, 1 - core, first, second)
        n = first * 4 + second
        send(part_ref.at[place_of(nx, nz, 1 - core)], sib.at[first, second], send_s.at[n], recv_s.at[n], sibling)
    gain_send(0, gain_part[...])

    def combine(first, second):
        n = first * 4 + second
        arrived(sib.at[first, second], recv_s.at[n])
        nx, nz = shifted(x, z, core, first, second)
        return part_ref[place_of(nx, nz, core)].astype(F32) + sib[first, second].astype(F32)

    for first in (2, 1, 3, 0):
        work[first, 2] = combine(first, 2).astype(BF16)
        for half in (0, 1):
            send(work.at[first, 2, half], half_b.at[first, half], send_hb.at[first, half], recv_hb.at[first, half], ring_b[half])
    gain_send(1, gain_sum(0))
    for first in (2, 1, 3, 0):
        for half, second in ((0, 1), (1, 3)):
            mine = combine(first, second)
            arrived(half_b.at[first, half], recv_hb.at[first, half])
            work[first, second] = mine.astype(BF16)
            work[first, second, half] = (mine[half] + half_b[first, half].astype(F32)).astype(BF16)
            send(work.at[first, second], full_b.at[first, half], send_fb.at[first, half], recv_fb.at[first, half], ring_b[half])
    gain_send(2, gain_sum(1))

    def settled(first):
        mine = combine(first, 0)
        for half in (0, 1):
            arrived(full_b.at[first, half], recv_fb.at[first, half])
            mine = mine + full_b[first, half].astype(F32)
        return mine

    work[2, 0] = settled(2).astype(BF16)
    for half in (0, 1):
        send(work.at[2, 0, half], half_a.at[half], send_a.at[half], recv_a.at[half], ring_a[half])
    gain_send(3, gain_sum(2))
    for half, first in ((0, 1), (1, 3)):
        mine = settled(first)
        arrived(half_a.at[half], recv_a.at[half])
        work[first, 0] = mine.astype(BF16)
        work[first, 0, half] = (mine[half] + half_a[half].astype(F32)).astype(BF16)
        send(work.at[first, 0], full_a.at[half], send_a.at[2 + half], recv_a.at[2 + half], ring_a[half])
    mine = settled(0)
    totals = gain_sum(3)
    gain = gain_ref[...]
    tower = lax.rem(z, 2)
    row = lax.broadcasted_iota(I32, (8, 128), 0)
    query_sum = jnp.sum(jnp.where(row == tower, totals, 0.0), axis=0, keepdims=True)
    key_sum = jnp.sum(jnp.where(row == 2 + tower, totals, 0.0), axis=0, keepdims=True)
    gain_out[0:1, :] = query_sum
    gain_out[1:2, :] = key_sum * scale / gain
    for half in (0, 1):
        arrived(full_a.at[half], recv_a.at[2 + half])
        mine = mine + full_a[half].astype(F32)
    value_out[...] = mine[1].astype(BF16)
    keys = key_ref[...].astype(F32)
    inverse = lax.rsqrt(jnp.mean(keys * keys, axis=-1, keepdims=True) + EPSILON)
    unit = keys * inverse
    e = mine[0] * scale * gain
    key_out[...] = (inverse * (e - unit * jnp.mean(e * unit, axis=-1, keepdims=True))).astype(BF16)
    for copy in started:
        copy.wait_send()


def reduced(part, gain_part, key_input, key_gain):
    rows, dim = key_input.shape
    whole = pl.BlockSpec(memory_space=VMEM)
    one = (2, rows, dim)
    return pl.pallas_call(
        reduce_kernel,
        out_shape=(
            jax.ShapeDtypeStruct((rows, dim), BF16),
            jax.ShapeDtypeStruct((rows, dim), BF16),
            jax.ShapeDtypeStruct((2, dim), F32),
        ),
        in_specs=[whole] * 4,
        out_specs=(whole,) * 3,
        scratch_shapes=[
            VMEM((4, 4, *one), BF16), VMEM((4, 4, *one), BF16), VMEM((4, *one), BF16), VMEM((4, 2, *one), BF16),
            VMEM(one, BF16), VMEM((2, *one), BF16), VMEM((4, 4, 8, dim), F32),
            DMA((16,)), DMA((16,)), DMA((4, 2)), DMA((4, 2)), DMA((4, 2)), DMA((4, 2)), DMA((4,)), DMA((4,)),
            DMA((4, 4)), DMA((4, 4)),
        ],
        compiler_params=pltpu.CompilerParams(collective_id=1, has_side_effects=True),
        name="reduce_keys",
    )(part, gain_part, key_input, key_gain)


def shards(
    query_input, key_input, value_input, output_grad, query_gain, key_gain, stripe_order, frame_index, cross_blocks
):
    order = jnp.pad(stripe_order, (0, 32))[None]
    frame = jnp.pad(frame_index, (48, 32), constant_values=-1)[None]
    cross = jnp.pad(cross_blocks, ((0, 0), (0, 32)))
    kv, lists = gathered(key_input, value_input, key_gain, order, frame, cross)
    query_grad, gain_part, part = attention(lists, query_input, output_grad, query_gain, kv, 768)
    key_grad, value_grad, gain_grads = reduced(part, gain_part, key_input, key_gain)
    return query_grad, key_grad, value_grad, gain_grads[:, None, :]


def solution(mesh):
    split = Mesh(mesh.devices.reshape(mesh.shape["heads"], mesh.shape["tower"], 2, 4, 2), AXES)
    in_specs = (
        P(TOWER_BLK, "heads"),
        P(TOWER_BLK, "heads"),
        P(TOWER_BLK, "heads"),
        P(TOWER_BLK, "heads"),
        P("tower", None),
        P("tower", None),
        P(),
        P(),
        P(),
    )
    out_specs = (
        P(TOWER_BLK, "heads"),
        P(TOWER_BLK, "heads"),
        P(TOWER_BLK, "heads"),
        P(None, "tower", None),
    )
    return jax.shard_map(shards, mesh=split, in_specs=in_specs, out_specs=out_specs, check_vma=False)
```

time: 375 us -> 88.1 us (0.23)
  matrix products: 139 us -> 0 us
  Pallas kernels: 0 us -> 79.2 us
  local copies, waits for them, and re-layouts: 78 us -> 6.74 us
  other arithmetic: 62.7 us -> 0 us
  waiting for transfers between devices: 53.2 us -> 0 us
  starting transfers between devices: 18.5 us -> 0 us
  blocking collectives: 15.6 us -> 0 us
    dot_general x112 -> x0, matrix products: 139 us -> none  [the longest x32 51.1 us: logits_of(): jnp.einsum('rghd,kgd->rghk', q_normed, keys, preferred_element_type=jnp.f...]
    pallas_call x0 -> x3, Pallas kernels: none -> 79.2 us  [the longest x1 27.7 us: reduced(): pl.pallas_call(reduce_kernel, out_shape=(jax.ShapeDtypeStruct((rows, dim)...]
    all_to_all x3 -> x0, waiting for transfers between devices: 53.2 us -> none  [the longest x2 29.5 us: sent_to_all(): lax.all_to_all(jnp.broadcast_to(array[None], (size, *array.shape)), axis,...]
    or x32 -> x0, other arithmetic: 25.2 us -> none  [allowed_pairs(): segment_open = (query_image[:, None] == key_image[None, :]) | opened]
    reduce_sum x24 -> x0, other arithmetic: 21.1 us -> none  [the longest x16 14.2 us: stats_step(): total = total * factor + jnp.sum(weights, axis=-1)]
    all_to_all x3 -> x0, starting transfers between devices: 18.5 us -> none  [the longest x2 14.8 us: sent_to_all(): lax.all_to_all(jnp.broadcast_to(array[None], (size, *array.shape)), axis,...]
    all_to_all x2 -> x0, blocking collectives: 15.6 us -> none  [the longest x1 8.28 us: sent_to_all(): lax.all_to_all(jnp.broadcast_to(array[None], (size, *array.shape)), axis,...]
    dynamic_update_slice x32 -> x0, local copies, waits for them, and re-layouts: 13.5 us -> none  [merged_step(): return (grad_q, lax.dynamic_update_slice_in_dim(grad_kv, block, offset, 0))]
  transfers between devices with their start and end apart: 3 -> 0, of which waited for: 3 -> 0; matrix products, arithmetic and copies ran while one was open for 1% -> 0% of each run, Pallas kernels for 0% -> 0%
where the time goes in v1:
time: 88.1 us; the launch traced here: 86.6 us
  Pallas kernels  79.2 us (90%)
  local copies, waits for them, and re-layouts  6.74 us (8%)
    pallas_call x1, Pallas kernels, reduced(): pl.pallas_call(reduce_kernel, out_shape=(jax.ShapeDtypeStruct((rows, dim)...  27.7 us
    pallas_call x1, Pallas kernels, gathered(): pl.pallas_call(gather_kernel, out_shape=(jax.ShapeDtypeStruct((32, 2, row...  26.4 us
    pallas_call x1, Pallas kernels, attention(): pl.pallas_call(functools.partial(attention_kernel, per_group, rows // SEG...  25.1 us
    unnamed x3, local copies, waits for them, and re-layouts  4.06 us

profile of v1, /device:TPU:1, one launch (start us, length us, event | category | flops | bytes accessed | tf_op | source)
XLA Modules:
  0.0 86.6 jit_solution(9863771732818191890)
XLA Ops:
  0.6 1.3 %pad_bitcast_fusion = (s32[1,128]{1,0:T(1,128)}, s32[1,128]{1,0:T(1,128)}) fusion(s32[48]{0:T(128)} %param.16, s32[96]{0:T(128)} %param.15), kind=kLoop, calls=%fused_computation | loop fusion | bytes 1600 | tf_op jit(solution)/shard_map/broadcast_in_dim | solution.py:513
  1.9 1.4 %pad.14.cross_ref = s32[96,128]{1,0:T(8,128)} pad(s32[96,96]{1,0:T(8,128)} %param.17, s32[]{:T(128)} %constant.0.clone.1), padding=0_0x0_32 | pad | bytes 86020 | tf_op jit(solution)/shard_map/jit(_pad)/pad | solution.py:514
  3.3 26.4 %gather_keys.1 = (bf16[32,2,192,128]{3,2,1,0:T(8,128)(2,1)}, s32[8,128]{1,0:T(8,128)}) custom-call(bf16[192,128]{1,0:T(8,128)(2,1)} %key_ref.3, bf16[192,128]{1,0:T(8,128)(2,1)} %value_ref.1, f32[1,128]{1,0:T(1,128)} %gain_ref.5, s32[1,128]{1,0:T(1,128)} %get-tuple-element.25.order_ref, s32[1,128]{1,0:T(1,128)} %get-tuple-element.24.frame_ref, ...), custom_call_target="tpu_custom_call" | custom-call | tf_op jit(solution)/shard_map/gather_keys/pallas_call | solution.py:182
  29.7 25.1 %attention.1 = (bf16[192,896]{1,0:T(8,128)(2,1)}, f32[8,128]{1,0:T(8,128)}, bf16[32,2,192,128]{3,2,1,0:T(8,128)(2,1)}) custom-call(s32[8,128]{1,0:T(8,128)} %get-tuple-element.12.list_ref, bf16[192,896]{1,0:T(8,128)(2,1)} %query_ref.1, bf16[192,896]{1,0:T(8,128)(2,1)} %grad_ref.1, f32[1,128]{1,0:T(1,128)} %gain_ref.4, bf16[12288,128]{1,0:T(8,128)(2,1)} %bitcast.8), custom_call_target="tpu_custom_call" | custom-call | tf_op jit(solution)/shard_map/attention/pallas_call | solution.py:348
  54.8 27.7 %reduce_keys.1 = (bf16[192,128]{1,0:T(8,128)(2,1)}, bf16[192,128]{1,0:T(8,128)(2,1)}, f32[2,128]{1,0:T(2,128)}) custom-call(bf16[32,2,192,128]{3,2,1,0:T(8,128)(2,1)} %get-tuple-element.15.part_ref, f32[8,128]{1,0:T(8,128)} %get-tuple-element.16.gain_part, bf16[192,128]{1,0:T(8,128)(2,1)} %key_ref.3, f32[1,128]{1,0:T(1,128)} %gain_ref.5), custom_call_target="tpu_custom_call" | custom-call | tf_op jit(solution)/shard_map/reduce_keys/pallas_call | solution.py:489
  82.5 1.4 %copy.17 = bf16[192,128]{1,0:T(8,128)(2,1)} copy(bf16[192,128]{1,0:T(8,128)(2,1)} %get-tuple-element.31) | data formatting | bytes 98304
  83.9 1.4 %copy.18 = bf16[192,128]{1,0:T(8,128)(2,1)} copy(bf16[192,128]{1,0:T(8,128)(2,1)} %get-tuple-element.32) | data formatting | bytes 98304
  85.4 1.2 %copy.19 = f32[2,1,128]{2,1,0:T(1,128)} copy(f32[2,1,128]{2,1,0:T(1,128)} %bitcast.9) | data formatting | bytes 2048

commit v2 on v1

--- a/solution.py
+++ b/solution.py
@@ -16,6 +16,11 @@
 NEGATIVE = -1e30
 LOG2E = 1.4426950408889634
 MESH = pl.DeviceIdType.MESH
+HBM = pl.BlockSpec(memory_space=pltpu.HBM)
+MIB = 1024 * 1024
+DIRECT_A, DIRECT_B, LATE = True, (2,), False
+SUM_A, SUM_B = True, ()
+MOST, CHUNKS, ROWS = 67_043_328, 32 * 2 * 192 * 128 * 2, 2 * 192 * 896 * 2
 VMEM = pltpu.VMEM
 DMA = pltpu.SemaphoreType.DMA
 F32, BF16, I32 = jnp.float32, jnp.bfloat16, jnp.int32
@@ -58,8 +63,9 @@
 
 
 def gather_kernel(
-    key_ref, value_ref, gain_ref, order_ref, frame_ref, cross_ref, all_ref, list_ref,
-    mine, own_sem, send_a, recv_a, send_b, recv_b, send_s, recv_s,
+    key_hbm, value_hbm, gain_hbm, order_hbm, frame_hbm, cross_hbm, query_hbm, grad_hbm, query_gain_hbm,
+    all_ref, list_ref, query_out, grad_out, query_gain_out,
+    key_ref, gain_ref, order_ref, frame_ref, cross_ref, mine, load_sem, own_sem, send_a, recv_a, send_b, recv_b, send_s, recv_s,
 ):
     y, x, z, core = position()
 
@@ -71,14 +77,32 @@
         nx, nz = shifted(x, z, core, first, second)
         return place_of(nx, nz, core)
 
+    loads = [
+        pltpu.make_async_copy(src, dst, load_sem.at[n])
+        for n, (src, dst) in enumerate((
+            (key_hbm, key_ref),
+            (gain_hbm, gain_ref),
+            (value_hbm, mine.at[1]),
+            (order_hbm, order_ref),
+            (frame_hbm, frame_ref),
+            (cross_hbm, cross_ref),
+            (query_hbm, query_out),
+            (grad_hbm, grad_out),
+            (query_gain_hbm, query_gain_out),
+        ))
+    ]
+    for load in loads:
+        load.start()
     sibling = device(y, x, z, 1 - core)
     ring_a = (target(1, 0), target(3, 0))
     ring_b = (target(0, 1), target(0, 3))
-    wait_all = meet((*ring_a, *ring_b, sibling))
+    far_a, far_b = target(2, 0), target(0, 2)
+    wait_all = meet((*ring_a, *ring_b, far_a, far_b, sibling))
+    loads[0].wait()
+    loads[1].wait()
     keys = key_ref[...].astype(F32)
     inverse = lax.rsqrt(jnp.mean(keys * keys, axis=-1, keepdims=True) + EPSILON)
     mine[0] = (keys * inverse * gain_ref[...]).astype(BF16)
-    mine[1] = value_ref[...]
     me = place_of(x, z, core)
     own = pltpu.make_async_copy(mine, all_ref.at[me], own_sem)
     started = []
@@ -95,22 +119,32 @@
         at = all_ref.at[chunk(first, 0)]
         send(src, at, send_b.at[first, 0], recv_b.at[first, 1], ring_b[0])
         send(src, at, send_b.at[first, 1], recv_b.at[first, 0], ring_b[1])
+        if first in DIRECT_B:
+            send(src, at, send_b.at[first, 2], recv_b.at[first, 2], far_b)
 
     def share(first, second, src):
         n = first * 4 + second
         send(src, all_ref.at[chunk(first, second)], send_s.at[n], recv_s.at[n], sibling)
 
+    loads[2].wait()
     wait_all()
     own.start()
     send(mine, all_ref.at[me], send_a.at[0], recv_a.at[1], ring_a[0])
     send(mine, all_ref.at[me], send_a.at[1], recv_a.at[0], ring_a[1])
-    spread(0, mine)
+    if DIRECT_A:
+        send(mine, all_ref.at[me], send_a.at[2], recv_a.at[2], far_a)
+    if not LATE:
+        spread(0, mine)
     share(0, 0, mine)
 
     lane = lax.broadcasted_iota(I32, (1, 128), 1)
     down = lax.broadcasted_iota(I32, (128, 128), 0)
     across = lax.broadcasted_iota(I32, (128, 128), 1)
-    order, frame = order_ref[...], frame_ref[...]
+    for load in loads[3:6]:
+        load.wait()
+    order = jnp.concatenate([order_ref[...], jnp.zeros((1, 32), I32)], axis=1)
+    frame = jnp.concatenate([frame_ref[...], jnp.zeros((1, 80), I32)], axis=1)
+    frame = jnp.where((lane >= 48) & (lane < 96), pltpu.roll(frame, 48, 1), -1)
     below = (across < down).astype(F32)
     start_of = (lax.shift_right_logical(down * 171, 9) * 384 + (down - 3 * lax.shift_right_logical(down * 171, 9)) * 64)
     image = me >= 16
@@ -123,7 +157,8 @@
         seen = jnp.sum(jnp.where(here, frame, 0), axis=-1, keepdims=True)
         same = (lane >= 48) == image
         near = (order <= slot) | ((frame == seen) & (seen >= 0))
-        opened = same | (cross_ref[pl.ds(block, 1), :] == 1)
+        crossing = jnp.concatenate([cross_ref[pl.ds(block, 1), :], jnp.zeros((1, 32), I32)], axis=1)
+        opened = same | (crossing == 1)
         others = (near & opened & (lane < 96) & (lane != block)).astype(F32)
         column = jnp.broadcast_to(others, (128, 128)).T
         at = dot(below, column, 1, 0).astype(I32) + 1
@@ -138,14 +173,16 @@
     def from_a(slot, first, half, to, forward_recv):
         at = all_ref.at[chunk(first, 0)]
         arrived(at, recv_a.at[slot])
-        send(at.at[half], at.at[half], send_a.at[2 + half], recv_a.at[forward_recv], to)
+        if not DIRECT_A:
+            send(at.at[half], at.at[half], send_a.at[2 + half], recv_a.at[forward_recv], to)
         spread(first, at)
         share(first, 0, at)
 
     def from_b(first, slot, second, half, to):
         at = all_ref.at[chunk(first, second)]
         arrived(at, recv_b.at[first, slot])
-        send(at.at[half], at.at[half], send_b.at[first, 2 + half], recv_b.at[first, 2 + half], to)
+        if first not in DIRECT_B:
+            send(at.at[half], at.at[half], send_b.at[first, 2 + half], recv_b.at[first, 2 + half], to)
         share(first, second, at)
 
     def both_b(first):
@@ -154,21 +191,34 @@
 
     from_a(0, 1, 0, ring_a[1], 2)
     from_a(1, 3, 1, ring_a[0], 3)
-    both_b(0)
+    if LATE:
+        spread(0, mine)
+    if not DIRECT_A:
+        both_b(0)
     at = all_ref.at[chunk(2, 0)]
-    arrived(at.at[0], recv_a.at[2])
-    arrived(at.at[1], recv_a.at[3])
+    if DIRECT_A:
+        arrived(at, recv_a.at[2])
+    else:
+        arrived(at.at[0], recv_a.at[2])
+        arrived(at.at[1], recv_a.at[3])
     spread(2, at)
     share(2, 0, at)
+    if DIRECT_A:
+        both_b(0)
     both_b(1)
     both_b(3)
     both_b(2)
     for first in (0, 1, 3, 2):
         at = all_ref.at[chunk(first, 2)]
-        arrived(at.at[0], recv_b.at[first, 2])
-        arrived(at.at[1], recv_b.at[first, 3])
+        if first in DIRECT_B:
+            arrived(at, recv_b.at[first, 2])
+        else:
+            arrived(at.at[0], recv_b.at[first, 2])
+            arrived(at.at[1], recv_b.at[first, 3])
         share(first, 2, at)
     own.wait()
+    for load in loads[6:]:
+        load.wait()
     for copy in started:
         copy.wait_send()
     for n in range(16):
@@ -176,20 +226,25 @@
         arrived(all_ref.at[place_of(nx, nz, 1 - core)], recv_s.at[n])
 
 
-def gathered(key_input, value_input, key_gain, order, frame, cross):
+def gathered(key_input, value_input, key_gain, order, frame, cross, query_input, output_grad, query_gain):
     rows, dim = key_input.shape
     whole = pl.BlockSpec(memory_space=VMEM)
     return pl.pallas_call(
         gather_kernel,
-        out_shape=(jax.ShapeDtypeStruct((32, 2, rows, dim), BF16), jax.ShapeDtypeStruct((8, 128), I32)),
-        in_specs=[whole] * 6,
-        out_specs=(pl.BlockSpec(memory_space=pl.ANY), whole),
+        out_shape=(
+            VMEM((32, 2, rows, dim), BF16), VMEM((8, 128), I32), VMEM(query_input.shape, BF16), VMEM(query_input.shape, BF16),
+            VMEM((1, dim), F32),
+        ),
+        in_specs=[HBM] * 9,
+        out_specs=(pl.BlockSpec(memory_space=pl.ANY), whole, *(pl.BlockSpec(memory_space=pl.ANY),) * 3),
         scratch_shapes=[
-            VMEM((2, rows, dim), BF16), DMA, DMA((4,)), DMA((4,)), DMA((4, 4)), DMA((4, 4)), DMA((16,)), DMA((16,)),
+            VMEM((rows, dim), BF16), VMEM((1, dim), F32), VMEM(order.shape, I32), VMEM(frame.shape, I32),
+            VMEM(cross.shape, I32), VMEM((2, rows, dim), BF16), DMA((9,)), DMA, DMA((4,)), DMA((4,)), DMA((4, 4)), DMA((4, 4)), DMA((16,)), DMA((16,)),
         ],
-        compiler_params=pltpu.CompilerParams(collective_id=0, has_side_effects=True),
+        compiler_params=pltpu.CompilerParams(collective_id=0, has_side_effects=True, vmem_limit_bytes=MOST - CHUNKS - ROWS - 16 * 1024),
+        cost_estimate=pl.CostEstimate(flops=0, bytes_accessed=60_000_000, transcendentals=0),
         name="gather_keys",
-    )(key_input, value_input, key_gain, order, frame, cross)
+    )(key_input, value_input, key_gain, order, frame, cross, query_input, output_grad, query_gain)
 
 
 def attention_kernel(
@@ -204,13 +259,12 @@
     scale = 1.0 / math.sqrt(dim)
     places = kv_ref.shape[0] // 384
     is_text = list_ref[3, 3] == 1
-    gain = gain_ref[...]
-
     def zero(i, _):
         acc[pl.ds(pl.multiple_of(i * 128, 128), 128), :] = jnp.zeros((128, dim), F32)
         return 0
 
     lax.fori_loop(0, places * 3, zero, 0)
+    gain = gain_ref[...]
     query_part = jnp.zeros((8, dim), F32)
 
     for b in range(blocks):
@@ -349,8 +403,8 @@
         functools.partial(attention_kernel, per_group, rows // SEGMENT, width),
         out_shape=(
             jax.ShapeDtypeStruct((rows, columns), BF16),
-            jax.ShapeDtypeStruct((8, 128), F32),
-            jax.ShapeDtypeStruct(kv.shape, BF16),
+            VMEM((8, 128), F32),
+            VMEM(kv.shape, BF16),
         ),
         in_specs=[pl.BlockSpec(memory_space=pltpu.SMEM)] + [whole] * 4,
         out_specs=(whole,) * 3,
@@ -360,14 +414,15 @@
             VMEM((stacked, 128), F32), VMEM((stacked, 128), F32), VMEM((stacked, 128), F32), VMEM((stacked, 128), F32),
             VMEM((flat, 128), F32),
         ],
-        compiler_params=pltpu.CompilerParams(vmem_limit_bytes=60 * 1024 * 1024),
+        compiler_params=pltpu.CompilerParams(vmem_limit_bytes=36 * MIB),
+        cost_estimate=pl.CostEstimate(flops=20_000_000_000, bytes_accessed=60_000_000, transcendentals=0),
         name="attention",
     )(lists, query_input, output_grad, query_gain, kv.reshape(flat, 128))
 
 
 def reduce_kernel(
-    part_ref, gain_part, key_ref, gain_ref, key_out, value_out, gain_out,
-    sib, work, half_b, full_b, half_a, full_a, sums,
+    part_ref, gain_part, key_hbm, gain_hbm, key_out, value_out, gain_out,
+    key_ref, gain_ref, load_sem, sib, work, half_b, full_b, half_a, full_a, sums,
     send_s, recv_s, send_hb, recv_hb, send_fb, recv_fb, send_a, recv_a, send_g, recv_g,
 ):
     y, x, z, core = position()
@@ -381,14 +436,16 @@
     ring_a = (target(1, 0), target(3, 0))
     ring_b = (target(0, 1), target(0, 3))
     lines = (
-        (y, 4, lambda n: device(n, x, z, core)),
-        (core, 2, lambda n: device(y, x, z, n)),
-        (x, 4, lambda n: device(y, n, z, core)),
-        (z, 4, lambda n: device(y, x, n, core)),
+        (y * 2 + core, 8, lambda n: device(lax.div(n, 2), x, z, lax.rem(n, 2))),
+        (x * 4 + z, 16, lambda n: device(y, lax.div(n, 4), lax.rem(n, 4), core)),
     )
-    peers = [sibling]
-    for at, size, of in lines[:1] + lines[2:]:
-        peers += [of(lax.rem(at + o, size)) for o in range(1, size)]
+    far_a, far_b = target(2, 0), target(0, 2)
+    peers = [of(lax.rem(at + o, size)) for at, size, of in lines for o in range(1, size)]
+    loads = [
+        pltpu.make_async_copy(key_hbm, key_ref, load_sem.at[0]), pltpu.make_async_copy(gain_hbm, gain_ref, load_sem.at[1])
+    ]
+    for load in loads:
+        load.start()
     meet(peers)()
     started = []
 
@@ -431,37 +488,48 @@
 
     for first in (2, 1, 3, 0):
         work[first, 2] = combine(first, 2).astype(BF16)
-        for half in (0, 1):
-            send(work.at[first, 2, half], half_b.at[first, half], send_hb.at[first, half], recv_hb.at[first, half], ring_b[half])
-    gain_send(1, gain_sum(0))
+        if first in SUM_B:
+            send(work.at[first, 2], half_b.at[first], send_hb.at[first, 0], recv_hb.at[first, 0], far_b)
+        else:
+            for half in (0, 1):
+                send(work.at[first, 2, half], half_b.at[first, half], send_hb.at[first, half], recv_hb.at[first, half], ring_b[half])
     for first in (2, 1, 3, 0):
         for half, second in ((0, 1), (1, 3)):
             mine = combine(first, second)
-            arrived(half_b.at[first, half], recv_hb.at[first, half])
             work[first, second] = mine.astype(BF16)
-            work[first, second, half] = (mine[half] + half_b[first, half].astype(F32)).astype(BF16)
+            if first not in SUM_B:
+                arrived(half_b.at[first, half], recv_hb.at[first, half])
+                work[first, second, half] = (mine[half] + half_b[first, half].astype(F32)).astype(BF16)
             send(work.at[first, second], full_b.at[first, half], send_fb.at[first, half], recv_fb.at[first, half], ring_b[half])
-    gain_send(2, gain_sum(1))
 
     def settled(first):
         mine = combine(first, 0)
+        if first in SUM_B:
+            arrived(half_b.at[first], recv_hb.at[first, 0])
+            mine = mine + half_b[first].astype(F32)
         for half in (0, 1):
             arrived(full_b.at[first, half], recv_fb.at[first, half])
             mine = mine + full_b[first, half].astype(F32)
         return mine
 
+    gain_send(1, gain_sum(0))
     work[2, 0] = settled(2).astype(BF16)
-    for half in (0, 1):
-        send(work.at[2, 0, half], half_a.at[half], send_a.at[half], recv_a.at[half], ring_a[half])
-    gain_send(3, gain_sum(2))
+    if SUM_A:
+        send(work.at[2, 0], half_a, send_a.at[0], recv_a.at[0], far_a)
+    else:
+        for half in (0, 1):
+            send(work.at[2, 0, half], half_a.at[half], send_a.at[half], recv_a.at[half], ring_a[half])
     for half, first in ((0, 1), (1, 3)):
         mine = settled(first)
-        arrived(half_a.at[half], recv_a.at[half])
         work[first, 0] = mine.astype(BF16)
-        work[first, 0, half] = (mine[half] + half_a[half].astype(F32)).astype(BF16)
+        if not SUM_A:
+            arrived(half_a.at[half], recv_a.at[half])
+            work[first, 0, half] = (mine[half] + half_a[half].astype(F32)).astype(BF16)
         send(work.at[first, 0], full_a.at[half], send_a.at[2 + half], recv_a.at[2 + half], ring_a[half])
     mine = settled(0)
-    totals = gain_sum(3)
+    totals = gain_sum(1)
+    for load in loads:
+        load.wait()
     gain = gain_ref[...]
     tower = lax.rem(z, 2)
     row = lax.broadcasted_iota(I32, (8, 128), 0)
@@ -469,6 +537,9 @@
     key_sum = jnp.sum(jnp.where(row == 2 + tower, totals, 0.0), axis=0, keepdims=True)
     gain_out[0:1, :] = query_sum
     gain_out[1:2, :] = key_sum * scale / gain
+    if SUM_A:
+        arrived(half_a, recv_a.at[0])
+        mine = mine + half_a[...].astype(F32)
     for half in (0, 1):
         arrived(full_a.at[half], recv_a.at[2 + half])
         mine = mine + full_a[half].astype(F32)
@@ -489,19 +560,20 @@
     return pl.pallas_call(
         reduce_kernel,
         out_shape=(
-            jax.ShapeDtypeStruct((rows, dim), BF16),
-            jax.ShapeDtypeStruct((rows, dim), BF16),
-            jax.ShapeDtypeStruct((2, dim), F32),
+            VMEM((rows, dim), BF16),
+            VMEM((rows, dim), BF16),
+            VMEM((2, dim), F32),
         ),
-        in_specs=[whole] * 4,
+        in_specs=[whole, whole, HBM, HBM],
         out_specs=(whole,) * 3,
         scratch_shapes=[
+            VMEM((rows, dim), BF16), VMEM((1, dim), F32), DMA((2,)),
             VMEM((4, 4, *one), BF16), VMEM((4, 4, *one), BF16), VMEM((4, *one), BF16), VMEM((4, 2, *one), BF16),
-            VMEM(one, BF16), VMEM((2, *one), BF16), VMEM((4, 4, 8, dim), F32),
+            VMEM(one, BF16), VMEM((2, *one), BF16), VMEM((2, 16, 8, dim), F32),
             DMA((16,)), DMA((16,)), DMA((4, 2)), DMA((4, 2)), DMA((4, 2)), DMA((4, 2)), DMA((4,)), DMA((4,)),
-            DMA((4, 4)), DMA((4, 4)),
+            DMA((2, 16)), DMA((2, 16)),
         ],
-        compiler_params=pltpu.CompilerParams(collective_id=1, has_side_effects=True),
+        compiler_params=pltpu.CompilerParams(collective_id=1, has_side_effects=True, vmem_limit_bytes=16 * MIB),
         name="reduce_keys",
     )(part, gain_part, key_input, key_gain)
 
@@ -509,11 +581,11 @@
 def shards(
     query_input, key_input, value_input, output_grad, query_gain, key_gain, stripe_order, frame_index, cross_blocks
 ):
-    order = jnp.pad(stripe_order, (0, 32))[None]
-    frame = jnp.pad(frame_index, (48, 32), constant_values=-1)[None]
-    cross = jnp.pad(cross_blocks, ((0, 0), (0, 32)))
-    kv, lists = gathered(key_input, value_input, key_gain, order, frame, cross)
-    query_grad, gain_part, part = attention(lists, query_input, output_grad, query_gain, kv, 768)
+    kv, lists, queries, grads, gain = gathered(
+        key_input, value_input, key_gain, stripe_order[None], frame_index[None], cross_blocks,
+        query_input, output_grad, query_gain,
+    )
+    query_grad, gain_part, part = attention(lists, queries, grads, gain, kv, 768)
     key_grad, value_grad, gain_grads = reduced(part, gain_part, key_input, key_gain)
     return query_grad, key_grad, value_grad, gain_grads[:, None, :]
 

time: 88.1 us -> 73.7 us (0.84)
  the two profiles are of different devices: /device:TPU:1 before, /device:TPU:32 now
where the time goes in v2:
time: 73.7 us; the launch traced here: 73.6 us
  Pallas kernels  71.1 us (96%)
  local copies, waits for them, and re-layouts  1.82 us (2%)
    pallas_call x1, Pallas kernels, attention(): pl.pallas_call(functools.partial(attention_kernel, per_group, rows // SEG...  29.2 us
    pallas_call x1, Pallas kernels, reduced(): pl.pallas_call(reduce_kernel, out_shape=(VMEM((rows, dim), BF16), VMEM((r...  23.3 us
    pallas_call x1, Pallas kernels, gathered(): pl.pallas_call(gather_kernel, out_shape=(VMEM((32, 2, rows, dim), BF16),...  18.5 us
    unnamed x7, local copies, waits for them, and re-layouts  1.82 us

profile of v2, /device:TPU:32, one launch (start us, length us, event | category | flops | bytes accessed | tf_op | source)
XLA Modules:
  0.0 73.6 jit_solution(9000316732754778990)
XLA Ops:
  0.6 18.5 %gather_keys.1 = (bf16[32,2,192,128]{3,2,1,0:T(8,128)(2,1)S(1)}, s32[8,128]{1,0:T(8,128)S(1)}, bf16[192,896]{1,0:T(8,128)(2,1)S(1)}, bf16[192,896]{1,0:T(8,128)(2,1)S(1)}, f32[1,128]{1,0:T(1,128)S(1)}) custom-call(bf16[192,128]{1,0:T(8,128)(2,1)} %key_hbm.3, bf16[192,128]{1,0:T(8,128)(2,1)} %value_hbm.1, f32[1,128]{1,0:T(1,128)} %gain_hbm.3, ...), custom_call_target="tpu_custom_call" | custom-call | bytes 60000000 | tf_op jit(solution)/shard_map/gather_keys/pallas_call | solution.py:232
  19.1 0.0 copy-start
  19.2 0.0 copy-start.1
  19.2 29.2 %attention.1 = (bf16[192,896]{1,0:T(8,128)(2,1)}, f32[8,128]{1,0:T(8,128)S(1)}, bf16[32,2,192,128]{3,2,1,0:T(8,128)(2,1)S(1)}) custom-call(s32[8,128]{1,0:T(8,128)S(1)} %get-tuple-element.15.list_ref, bf16[192,896]{1,0:T(8,128)(2,1)S(1)} %get-tuple-element.16.query_ref, bf16[192,896]{1,0:T(8,128)(2,1)S(1)} %get-tuple-element.17.grad_ref, ...), custom_call_target="tpu_custom_call" | custom-call | flops 20000000000 | bytes 60000000 | tf_op jit(solution)/shard_map/attention/pallas_call | solution.py:402
  48.4 0.0 copy-done
  48.4 0.0 copy-done.1
  48.4 23.3 %reduce_keys.1 = (bf16[192,128]{1,0:T(8,128)(2,1)S(1)}, bf16[192,128]{1,0:T(8,128)(2,1)S(1)}, f32[2,128]{1,0:T(2,128)S(1)}) custom-call(bf16[32,2,192,128]{3,2,1,0:T(8,128)(2,1)S(1)} %get-tuple-element.21.part_ref, f32[8,128]{1,0:T(8,128)S(1)} %get-tuple-element.22.gain_part, bf16[192,128]{1,0:T(8,128)(2,1)S(1)} %copy-done, f32[1,128]{1,0:T(1,128)S(1)} %copy-done.1), custom_call_target="tpu_custom_call" | custom-call | tf_op jit(solution)/shard_map/reduce_keys/pallas_call | solution.py:560
  71.8 0.6 copy.17
  72.4 0.6 copy.19
  73.0 0.6 copy.18
Async XLA Ops:
  19.1 29.3 %copy-start = (bf16[192,128]{1,0:T(8,128)(2,1)S(1)}, bf16[192,128]{1,0:T(8,128)(2,1)}, u32[]{:S(2)}) copy-start(bf16[192,128]{1,0:T(8,128)(2,1)} %key_hbm.3) | copy-start | bytes 147460
  19.2 29.3 %copy-start.1 = (f32[1,128]{1,0:T(1,128)S(1)}, f32[1,128]{1,0:T(1,128)}, u32[]{:S(2)}) copy-start(f32[1,128]{1,0:T(1,128)} %gain_hbm.3) | copy-start | bytes 1540

commit v3 on v2

--- a/solution.py
+++ b/solution.py
@@ -15,6 +15,7 @@
 EPSILON = 1e-06
 NEGATIVE = -1e30
 LOG2E = 1.4426950408889634
+WIDE, NARROW, LANES = 24, 12, 256
 MESH = pl.DeviceIdType.MESH
 HBM = pl.BlockSpec(memory_space=pltpu.HBM)
 MIB = 1024 * 1024
@@ -248,174 +249,229 @@
 
 
 def attention_kernel(
-    per_group, blocks, width, list_ref, query_ref, grad_ref, gain_ref, kv_ref,
+    per_group, blocks, list_ref, query_ref, grad_ref, gain_ref, kv_ref,
     out_ref, gain_out, part_ref,
-    qn, dop, s_ref, w_ref, m_ref, l_ref, o_ref, dq_ref, acc,
+    qn, qt, dop, dot_t, s_ref, w_ref, m_ref, l_ref, o_ref, acc,
 ):
     dim = 128
     rows = SEGMENT * per_group
-    per = width // SEGMENT
     log_scale = LOG2E / math.sqrt(dim)
     scale = 1.0 / math.sqrt(dim)
     places = kv_ref.shape[0] // 384
     is_text = list_ref[3, 3] == 1
+    gain = gain_ref[...]
+
     def zero(i, _):
-        acc[pl.ds(pl.multiple_of(i * 128, 128), 128), :] = jnp.zeros((128, dim), F32)
+        acc[i] = jnp.zeros((dim, 128), F32)
         return 0
 
     lax.fori_loop(0, places * 3, zero, 0)
-    gain = gain_ref[...]
-    query_part = jnp.zeros((8, dim), F32)
-
-    for b in range(blocks):
-        count = list_ref[3, b]
-        rest = lax.rem(count - 1, per)
-        groups = lax.div(count - 1, per)
+
+    def one_block(b, parts):
+        query_part, all_part = parts
+        base = pl.multiple_of(b * SEGMENT, SEGMENT)
+        count = list_ref[3, b] - 1
+        wide = lax.div(count, WIDE)
+        small = lax.div(lax.rem(count, WIDE), NARROW)
+        rest = lax.rem(count, NARROW)
         for h in range(per_group):
-            q = query_ref[b * SEGMENT : (b + 1) * SEGMENT, h * dim : (h + 1) * dim].astype(F32)
+            q = query_ref[pl.ds(base, SEGMENT), h * dim : (h + 1) * dim].astype(F32)
             inverse = lax.rsqrt(jnp.mean(q * q, axis=-1, keepdims=True) + EPSILON)
             qn[h * SEGMENT : (h + 1) * SEGMENT, :] = (q * inverse * gain).astype(BF16)
+        qt[...] = qn[...].astype(F32).T.astype(BF16)
         m_ref[...] = jnp.full_like(m_ref, NEGATIVE)
         l_ref[...] = jnp.zeros_like(l_ref)
         o_ref[...] = jnp.zeros_like(o_ref)
-        dq_ref[...] = jnp.zeros_like(dq_ref)
-
-        def starts(g):
-            out = []
-            for j in range(per):
-                if isinstance(g, int):
-                    p = 0 if j == 0 else jnp.where(j <= rest, j, 0)
-                else:
-                    p = 1 + rest + (g - 1) * per + j
-                out.append(pl.multiple_of(list_ref[b, p], SEGMENT))
-            return out
+
+        def starts(first, size):
+            return [pl.multiple_of(list_ref[b, first + j], SEGMENT) for j in range(size)]
+
+        def first_starts():
+            ps = [0] + [jnp.where(j <= rest, j, 0) for j in range(1, NARROW)]
+            return [pl.multiple_of(list_ref[b, p], SEGMENT) for p in ps]
 
         def tile(at, offset):
             return jnp.concatenate([kv_ref[pl.ds(s + offset, SEGMENT), :] for s in at], axis=0)
 
-        def logits(g, at, masked):
-            s = dot(qn[...], tile(at, 0), 1, 1)
+        def number(start):
+            return lax.div(start, 384) * 3 + lax.div(lax.rem(start, 384), SEGMENT)
+
+        def logits(slot, at, masked):
+            width = len(at) * SEGMENT
+            s = dot(qn[...], tile(at, 0), 1, 1) * log_scale
             if masked:
                 lane = lax.broadcasted_iota(I32, (rows, width), 1)
                 row = lax.broadcasted_iota(I32, (rows, width), 0)
                 limit = lax.rem(row, SEGMENT) + jnp.where(is_text, 0, SEGMENT)
                 ok = (lane < (rest + 1) * SEGMENT) & ((lane >= SEGMENT) | (lane <= limit))
                 s = jnp.where(ok, s, NEGATIVE)
-            s_ref[g] = s
             top = m_ref[...]
             for t in range(width // 128):
                 top = jnp.maximum(top, s[:, t * 128 : (t + 1) * 128])
             m_ref[...] = top
-
-        def weights(g, at):
+            for t in range(width // LANES):
+                s_ref[slot + t] = s[:, t * LANES : (t + 1) * LANES]
+
+        def weights(slot, at):
             top = m_ref[...]
             total = l_ref[...]
-            parts = []
-            for t in range(width // 128):
-                w = jnp.exp2((s_ref[g, :, t * 128 : (t + 1) * 128] - top) * log_scale)
-                total = total + w
-                parts.append(w.astype(BF16))
+            out = o_ref[...]
+            tiles = len(at) * SEGMENT // LANES
+            each = LANES // SEGMENT
+            values = [tile(at[u * each : (u + 1) * each], 192).T for u in range(tiles)]
+            ready = []
+            for u in range(tiles + 1):
+                if u < tiles:
+                    parts = []
+                    for t in range(LANES // 128):
+                        w = jnp.exp2(s_ref[slot + u, :, t * 128 : (t + 1) * 128] - top)
+                        total = total + w
+                        parts.append(w.astype(BF16))
+                    w = jnp.concatenate(parts, axis=1)
+                    w_ref[slot + u] = w
+                    ready.append(w)
+                if u > 0:
+                    out = out + dot(values[u - 1], ready[u - 1], 1, 1)
             l_ref[...] = total
-            w = jnp.concatenate(parts, axis=1)
-            w_ref[g] = w
-            o_ref[...] += dot(w, tile(at, 192), 1, 0)
-
-        def slopes(g, at):
-            keys = tile(at, 0)
-            pushes = dot(dop[...], tile(at, 192), 1, 1)
+            o_ref[...] = out
+
+        def slopes(slot, at):
             delta = m_ref[...]
-            w = w_ref[g]
-            parts = []
-            for t in range(width // 128):
-                sl = slice(t * 128, (t + 1) * 128)
-                parts.append((w[:, sl].astype(F32) * (pushes[:, sl] - delta)).astype(BF16))
-            ds = jnp.concatenate(parts, axis=1)
-            dq_ref[...] += dot(ds, keys, 1, 0)
-            dk = dot(ds, qn[...], 0, 0)
-            dv = dot(w, dop[...], 0, 0)
-            for j in range(per):
-                sl = slice(j * SEGMENT, (j + 1) * SEGMENT)
-                acc[pl.ds(at[j], SEGMENT), :] += dk[sl]
-                acc[pl.ds(at[j] + 192, SEGMENT), :] += dv[sl]
+            low = lax.broadcasted_iota(I32, (dim, 128), 1) < SEGMENT
+            tiles = len(at) * SEGMENT // LANES
+            each = LANES // SEGMENT
+            here = [at[u * each : (u + 1) * each] for u in range(tiles)]
+            keys = [tile(h, 0).T for h in here]
+            pushes, ds, done = {}, {}, {}
+            grad_q = o_ref[...]
+            for step in range(tiles + 2):
+                if step < tiles:
+                    pushes[step] = dot(dop[...], tile(here[step], 192), 1, 1)
+                u = step - 1
+                if 0 <= u < tiles:
+                    w = w_ref[slot + u]
+                    parts = []
+                    for t in range(LANES // 128):
+                        sl = slice(t * 128, (t + 1) * 128)
+                        parts.append((w[:, sl].astype(F32) * (pushes[u][:, sl] - delta)).astype(BF16))
+                    d = jnp.concatenate(parts, axis=1)
+                    grad_q = grad_q + dot(keys[u], d, 1, 1)
+                    done[u] = dot(qt[...], d, 1, 0), dot(dot_t[...], w, 1, 0)
+                u = step - 2
+                if 0 <= u < tiles:
+                    dk, dv = done[u]
+                    for t in range(LANES // 128):
+                        sl = slice(t * 128, (t + 1) * 128)
+                        k2, v2 = dk[:, sl], dv[:, sl]
+                        acc[number(here[u][2 * t])] += jnp.where(low, k2, pltpu.roll(v2, SEGMENT, 1))
+                        acc[number(here[u][2 * t + 1])] += jnp.where(low, pltpu.roll(k2, SEGMENT, 1), v2)
+            o_ref[...] = grad_q
 
         def over(step):
-            def body(g, _):
-                step(g, starts(g))
+            def narrow(g, _):
+                step((1 + g) * (NARROW * SEGMENT // LANES), starts(1 + rest + g * NARROW, NARROW))
                 return 0
 
-            lax.fori_loop(1, groups + 1, body, 0)
-
-        logits(0, starts(0), True)
-        over(lambda g, at: logits(g, at, False))
+            def broad(g, _):
+                step(
+                    (1 + small) * (NARROW * SEGMENT // LANES) + g * (WIDE * SEGMENT // LANES),
+                    starts(1 + rest + small * NARROW + g * WIDE, WIDE),
+                )
+                return 0
+
+            lax.fori_loop(0, small, narrow, 0)
+            lax.fori_loop(0, wide, broad, 0)
+
+        logits(0, first_starts(), True)
+        over(lambda slot, at: logits(slot, at, False))
         m_ref[...] = jnp.broadcast_to(jnp.max(m_ref[...], axis=-1, keepdims=True), m_ref.shape)
-        weights(0, starts(0))
+        weights(0, first_starts())
         over(weights)
         total = jnp.sum(l_ref[...], axis=-1, keepdims=True)
         over_total = 1.0 / total
-        output = (o_ref[...] / total).astype(BF16).astype(F32)
+        output = (o_ref[...].T / total).astype(BF16).astype(F32)
+        o_ref[...] = jnp.zeros_like(o_ref)
         for h in range(per_group):
             sl = slice(h * SEGMENT, (h + 1) * SEGMENT)
-            g = grad_ref[b * SEGMENT : (b + 1) * SEGMENT, h * dim : (h + 1) * dim].astype(F32)
+            g = grad_ref[pl.ds(base, SEGMENT), h * dim : (h + 1) * dim].astype(F32)
             g = (g * over_total[sl]).astype(BF16)
             dop[sl, :] = g
             delta = jnp.sum(g.astype(F32) * output[sl], axis=-1, keepdims=True)
             m_ref[sl, :] = jnp.broadcast_to(delta, (SEGMENT, 128))
-        slopes(0, starts(0))
+        dot_t[...] = dop[...].astype(F32).T.astype(BF16)
+        slopes(0, first_starts())
         over(slopes)
+        raw = o_ref[...].T
         for h in range(per_group):
             sl = slice(h * SEGMENT, (h + 1) * SEGMENT)
-            q = query_ref[b * SEGMENT : (b + 1) * SEGMENT, h * dim : (h + 1) * dim].astype(F32)
+            q = query_ref[pl.ds(base, SEGMENT), h * dim : (h + 1) * dim].astype(F32)
             inverse = lax.rsqrt(jnp.mean(q * q, axis=-1, keepdims=True) + EPSILON)
             unit = q * inverse
-            grad = dq_ref[sl, :] * scale
+            grad = raw[sl] * scale
             e = grad * gain
             dq = inverse * (e - unit * jnp.mean(e * unit, axis=-1, keepdims=True))
-            out_ref[b * SEGMENT : (b + 1) * SEGMENT, h * dim : (h + 1) * dim] = dq.astype(BF16)
+            out_ref[pl.ds(base, SEGMENT), h * dim : (h + 1) * dim] = dq.astype(BF16)
             query_part = query_part + jnp.sum((grad * unit).reshape(SEGMENT // 8, 8, dim), axis=0)
+            terms = raw[sl] * qn[sl, :].astype(F32)
+            all_part = all_part + jnp.sum(terms.reshape(SEGMENT // 8, 8, dim), axis=0)
+        return query_part, all_part
+
+    none = jnp.zeros((8, dim), F32)
+    query_part, all_part = lax.fori_loop(0, blocks, one_block, (none, none))
 
     def finish(i, part):
         at = pl.multiple_of(i * 384, 384)
-        mine = acc[pl.ds(at, 384), :]
-        part_ref[i, 0] = mine[:192].astype(BF16)
-        part_ref[i, 1] = mine[192:].astype(BF16)
-        terms = mine[:192] * kv_ref[pl.ds(at, 192), :].astype(F32)
-        return part + jnp.sum(terms.reshape(24, 8, dim), axis=0)
-
-    text = lax.fori_loop(0, places // 2, finish, jnp.zeros((8, dim), F32))
-    image = lax.fori_loop(places // 2, places, finish, jnp.zeros((8, dim), F32))
+        mine = [acc[i * 3 + j].astype(BF16) for j in range(3)]
+        keys = []
+        for j in range(3):
+            part_ref[i, j * dim : (j + 1) * dim, :] = mine[j]
+            keys.append(kv_ref[pl.ds(at + j * SEGMENT, SEGMENT), :])
+            keys.append(jnp.zeros_like(keys[-1]))
+        part = part + dot(jnp.concatenate(mine, axis=1), jnp.concatenate(keys, axis=0), 1, 0)
+        return part
+
+    text = lax.fori_loop(0, places // 2, finish, jnp.zeros((dim, dim), F32), unroll=4)
+
+    def store(i, _):
+        for j in range(3):
+            part_ref[i, j * dim : (j + 1) * dim, :] = acc[i * 3 + j].astype(BF16)
+        return 0
+
+    lax.fori_loop(places // 2, places, store, 0)
+    diagonal = lax.broadcasted_iota(I32, (dim, dim), 0) == lax.broadcasted_iota(I32, (dim, dim), 1)
+    text_sum = jnp.sum(jnp.where(diagonal, text, 0.0), axis=0, keepdims=True)
+    image_sum = jnp.sum(all_part, axis=0, keepdims=True) - text_sum
     query_sum = jnp.sum(query_part, axis=0, keepdims=True)
     row = lax.broadcasted_iota(I32, (8, dim), 0)
     filled = jnp.where(row == jnp.where(is_text, 0, 1), query_sum, 0.0)
-    filled = jnp.where(row == 2, jnp.sum(text, axis=0, keepdims=True), filled)
-    gain_out[...] = jnp.where(row == 3, jnp.sum(image, axis=0, keepdims=True), filled)
-
-
-def attention(lists, query_input, output_grad, query_gain, kv, width):
+    filled = jnp.where(row == 2, text_sum, filled)
+    gain_out[...] = jnp.where(row == 3, image_sum, filled)
+
+
+def attention(lists, query_input, output_grad, query_gain, kv):
     rows, columns = query_input.shape
     per_group = columns // 128
     stacked = SEGMENT * per_group
     segments = kv.shape[0] * 3
-    per = width // SEGMENT
-    groups = (segments + per - 1) // per + 1
+    slots = (segments + NARROW) * SEGMENT // LANES
     flat = kv.shape[0] * 384
     whole = pl.BlockSpec(memory_space=VMEM)
     return pl.pallas_call(
-        functools.partial(attention_kernel, per_group, rows // SEGMENT, width),
+        functools.partial(attention_kernel, per_group, rows // SEGMENT),
         out_shape=(
             jax.ShapeDtypeStruct((rows, columns), BF16),
             VMEM((8, 128), F32),
-            VMEM(kv.shape, BF16),
+            VMEM((kv.shape[0], 384, 128), BF16),
         ),
         in_specs=[pl.BlockSpec(memory_space=pltpu.SMEM)] + [whole] * 4,
         out_specs=(whole,) * 3,
         scratch_shapes=[
-            VMEM((stacked, 128), BF16), VMEM((stacked, 128), BF16),
-            VMEM((groups, stacked, width), F32), VMEM((groups, stacked, width), BF16),
-            VMEM((stacked, 128), F32), VMEM((stacked, 128), F32), VMEM((stacked, 128), F32), VMEM((stacked, 128), F32),
-            VMEM((flat, 128), F32),
+            VMEM((stacked, 128), BF16), VMEM((128, stacked), BF16), VMEM((stacked, 128), BF16), VMEM((128, stacked), BF16),
+            VMEM((slots, stacked, LANES), F32), VMEM((slots, stacked, LANES), BF16),
+            VMEM((stacked, 128), F32), VMEM((stacked, 128), F32), VMEM((128, stacked), F32),
+            VMEM((segments, 128, 128), F32),
         ],
-        compiler_params=pltpu.CompilerParams(vmem_limit_bytes=36 * MIB),
-        cost_estimate=pl.CostEstimate(flops=20_000_000_000, bytes_accessed=60_000_000, transcendentals=0),
+        compiler_params=pltpu.CompilerParams(vmem_limit_bytes=40 * MIB),
         name="attention",
     )(lists, query_input, output_grad, query_gain, kv.reshape(flat, 128))
 
@@ -543,11 +599,15 @@
     for half in (0, 1):
         arrived(full_a.at[half], recv_a.at[2 + half])
         mine = mine + full_a[half].astype(F32)
-    value_out[...] = mine[1].astype(BF16)
+    blocks = jnp.concatenate([mine[0], mine[1]], axis=0)
+    blocks = [blocks[j * 128 : (j + 1) * 128].T for j in range(3)]
+    grad_keys = jnp.concatenate([block[:SEGMENT] for block in blocks], axis=0)
+    grad_values = jnp.concatenate([block[SEGMENT:] for block in blocks], axis=0)
+    value_out[...] = grad_values.astype(BF16)
     keys = key_ref[...].astype(F32)
     inverse = lax.rsqrt(jnp.mean(keys * keys, axis=-1, keepdims=True) + EPSILON)
     unit = keys * inverse
-    e = mine[0] * scale * gain
+    e = grad_keys * scale * gain
     key_out[...] = (inverse * (e - unit * jnp.mean(e * unit, axis=-1, keepdims=True))).astype(BF16)
     for copy in started:
         copy.wait_send()
@@ -585,8 +645,8 @@
         key_input, value_input, key_gain, stripe_order[None], frame_index[None], cross_blocks,
         query_input, output_grad, query_gain,
     )
-    query_grad, gain_part, part = attention(lists, queries, grads, gain, kv, 768)
-    key_grad, value_grad, gain_grads = reduced(part, gain_part, key_input, key_gain)
+    query_grad, gain_part, part = attention(lists, queries, grads, gain, kv)
+    key_grad, value_grad, gain_grads = reduced(part.reshape(kv.shape), gain_part, key_input, key_gain)
     return query_grad, key_grad, value_grad, gain_grads[:, None, :]
 
 

time: 73.7 us -> 71.7 us (0.973)
  the two profiles are of different devices: /device:TPU:32 before, /device:TPU:1 now
where the time goes in v3:
time: 71.7 us; the launch traced here: 72.5 us
  Pallas kernels  70 us (98%)
  local copies, waits for them, and re-layouts  1.81 us (3%)
    pallas_call x1, Pallas kernels, reduced(): pl.pallas_call(reduce_kernel, out_shape=(VMEM((rows, dim), BF16), VMEM((r...  25.1 us
    pallas_call x1, Pallas kernels, attention(): pl.pallas_call(functools.partial(attention_kernel, per_group, rows // SEG...  23.6 us
    pallas_call x1, Pallas kernels, gathered(): pl.pallas_call(gather_kernel, out_shape=(VMEM((32, 2, rows, dim), BF16),...  21.3 us
    unnamed x7, local copies, waits for them, and re-layouts  1.81 us

profile of v3, /device:TPU:1, one launch (start us, length us, event | category | flops | bytes accessed | tf_op | source)
XLA Modules:
  0.0 72.5 jit_solution(7748629448636060368)
XLA Ops:
  0.6 0.0 copy-start.1
  0.6 21.3 %gather_keys.1 = (bf16[32,2,192,128]{3,2,1,0:T(8,128)(2,1)S(1)}, s32[8,128]{1,0:T(8,128)S(1)}, bf16[192,896]{1,0:T(8,128)(2,1)S(1)}, bf16[192,896]{1,0:T(8,128)(2,1)S(1)}, f32[1,128]{1,0:T(1,128)S(1)}) custom-call(bf16[192,128]{1,0:T(8,128)(2,1)} %key_hbm.3, bf16[192,128]{1,0:T(8,128)(2,1)} %value_hbm.1, f32[1,128]{1,0:T(1,128)} %gain_hbm.3, ...), custom_call_target="tpu_custom_call" | custom-call | bytes 60000000 | tf_op jit(solution)/shard_map/gather_keys/pallas_call | solution.py:233
  21.9 0.0 copy-start
  21.9 23.6 %attention.1 = (bf16[192,896]{1,0:T(8,128)(2,1)}, f32[8,128]{1,0:T(8,128)S(1)}, bf16[32,384,128]{2,1,0:T(8,128)(2,1)S(1)}) custom-call(s32[8,128]{1,0:T(8,128)S(1)} %get-tuple-element.15.list_ref, bf16[192,896]{1,0:T(8,128)(2,1)S(1)} %get-tuple-element.16.query_ref, bf16[192,896]{1,0:T(8,128)(2,1)S(1)} %get-tuple-element.17.grad_ref, ...), custom_call_target="tpu_custom_call" | custom-call | tf_op jit(solution)/shard_map/attention/pallas_call | solution.py:459
  45.5 0.0 copy-done.1
  45.5 0.0 copy-done
  45.5 25.1 %reduce_keys.1 = (bf16[192,128]{1,0:T(8,128)(2,1)S(1)}, bf16[192,128]{1,0:T(8,128)(2,1)S(1)}, f32[2,128]{1,0:T(2,128)S(1)}) custom-call(bf16[32,2,192,128]{3,2,1,0:T(8,128)(2,1)S(1)} %bitcast.9, f32[8,128]{1,0:T(8,128)S(1)} %get-tuple-element.22.gain_part, bf16[192,128]{1,0:T(8,128)(2,1)S(1)} %copy-done, f32[1,128]{1,0:T(1,128)S(1)} %copy-done.1), custom_call_target="tpu_custom_call" | custom-call | tf_op jit(solution)/shard_map/reduce_keys/pallas_call | solution.py:620
  70.7 0.6 copy.17
  71.3 0.6 copy.19
  71.9 0.6 copy.18
Async XLA Ops:
  0.6 44.9 %copy-start.1 = (f32[1,128]{1,0:T(1,128)S(1)}, f32[1,128]{1,0:T(1,128)}, u32[]{:S(2)}) copy-start(f32[1,128]{1,0:T(1,128)} %gain_hbm.3) | copy-start | bytes 1540
  21.9 23.6 %copy-start = (bf16[192,128]{1,0:T(8,128)(2,1)S(1)}, bf16[192,128]{1,0:T(8,128)(2,1)}, u32[]{:S(2)}) copy-start(bf16[192,128]{1,0:T(8,128)(2,1)} %key_hbm.3) | copy-start | bytes 147460

commit v4 on v3

--- a/solution.py
+++ b/solution.py
@@ -15,13 +15,14 @@
 EPSILON = 1e-06
 NEGATIVE = -1e30
 LOG2E = 1.4426950408889634
-WIDE, NARROW, LANES = 24, 12, 256
+WIDE, NARROW, SMALL, LANES = 24, 12, 4, 256
 MESH = pl.DeviceIdType.MESH
 HBM = pl.BlockSpec(memory_space=pltpu.HBM)
 MIB = 1024 * 1024
 DIRECT_A, DIRECT_B, LATE = True, (2,), False
 SUM_A, SUM_B = True, ()
-MOST, CHUNKS, ROWS = 67_043_328, 32 * 2 * 192 * 128 * 2, 2 * 192 * 896 * 2
+STACKED = 448
+MOST, CHUNKS, ROWS, SUMS = 67_043_328, 32 * 2 * 192 * 128 * 2, 3 * 192 * 896 * 2 + 3 * 128 * 512 * 2, 96 * 128 * 128 * 4
 VMEM = pltpu.VMEM
 DMA = pltpu.SemaphoreType.DMA
 F32, BF16, I32 = jnp.float32, jnp.bfloat16, jnp.int32
@@ -65,7 +66,7 @@
 
 def gather_kernel(
     key_hbm, value_hbm, gain_hbm, order_hbm, frame_hbm, cross_hbm, query_hbm, grad_hbm, query_gain_hbm,
-    all_ref, list_ref, query_out, grad_out, query_gain_out,
+    all_ref, list_ref, query_out, grad_out, query_gain_out, qn_out, qt_out, acc_out,
     key_ref, gain_ref, order_ref, frame_ref, cross_ref, mine, load_sem, own_sem, send_a, recv_a, send_b, recv_b, send_s, recv_s,
 ):
     y, x, z, core = position()
@@ -171,6 +172,23 @@
         counts = jnp.where(lane == b, count, counts)
     list_ref[3:4, :] = counts
 
+    for load in loads[6:]:
+        load.wait()
+    query_gain = query_gain_out[...]
+    per_group = query_out.shape[1] // 128
+    for b in range(3):
+        for h in range(per_group):
+            q = query_out[b * SEGMENT : (b + 1) * SEGMENT, h * 128 : (h + 1) * 128].astype(F32)
+            inverse = lax.rsqrt(jnp.mean(q * q, axis=-1, keepdims=True) + EPSILON)
+            qn_out[b, h * SEGMENT : (h + 1) * SEGMENT, :] = (q * inverse * query_gain).astype(BF16)
+        qt_out[b] = qn_out[b].astype(F32).T.astype(BF16)
+
+    def clear(i, _):
+        acc_out[i] = jnp.zeros((128, 128), F32)
+        return 0
+
+    lax.fori_loop(0, acc_out.shape[0], clear, 0)
+
     def from_a(slot, first, half, to, forward_recv):
         at = all_ref.at[chunk(first, 0)]
         arrived(at, recv_a.at[slot])
@@ -218,8 +236,6 @@
             arrived(at.at[1], recv_b.at[first, 3])
         share(first, 2, at)
     own.wait()
-    for load in loads[6:]:
-        load.wait()
     for copy in started:
         copy.wait_send()
     for n in range(16):
@@ -234,24 +250,24 @@
         gather_kernel,
         out_shape=(
             VMEM((32, 2, rows, dim), BF16), VMEM((8, 128), I32), VMEM(query_input.shape, BF16), VMEM(query_input.shape, BF16),
-            VMEM((1, dim), F32),
+            VMEM((1, dim), F32), VMEM((3, STACKED, dim), BF16), VMEM((3, dim, STACKED), BF16), VMEM((96, dim, 128), F32),
         ),
         in_specs=[HBM] * 9,
-        out_specs=(pl.BlockSpec(memory_space=pl.ANY), whole, *(pl.BlockSpec(memory_space=pl.ANY),) * 3),
+        out_specs=(pl.BlockSpec(memory_space=pl.ANY), whole, *(whole,) * 6),
         scratch_shapes=[
             VMEM((rows, dim), BF16), VMEM((1, dim), F32), VMEM(order.shape, I32), VMEM(frame.shape, I32),
             VMEM(cross.shape, I32), VMEM((2, rows, dim), BF16), DMA((9,)), DMA, DMA((4,)), DMA((4,)), DMA((4, 4)), DMA((4, 4)), DMA((16,)), DMA((16,)),
         ],
-        compiler_params=pltpu.CompilerParams(collective_id=0, has_side_effects=True, vmem_limit_bytes=MOST - CHUNKS - ROWS - 16 * 1024),
+        compiler_params=pltpu.CompilerParams(collective_id=0, has_side_effects=True, vmem_limit_bytes=MOST - CHUNKS - ROWS - SUMS - 24 * 1024),
         cost_estimate=pl.CostEstimate(flops=0, bytes_accessed=60_000_000, transcendentals=0),
         name="gather_keys",
     )(key_input, value_input, key_gain, order, frame, cross, query_input, output_grad, query_gain)
 
 
 def attention_kernel(
-    per_group, blocks, list_ref, query_ref, grad_ref, gain_ref, kv_ref,
-    out_ref, gain_out, part_ref,
-    qn, qt, dop, dot_t, s_ref, w_ref, m_ref, l_ref, o_ref, acc,
+    per_group, blocks, list_ref, query_ref, grad_ref, gain_ref, kv_ref, qn_ref, qt_ref, clear_ref,
+    out_ref, gain_out, part_ref, acc,
+    dop, dot_t, s_ref, w_ref, m_ref, l_ref, o_ref,
 ):
     dim = 128
     rows = SEGMENT * per_group
@@ -261,12 +277,6 @@
     is_text = list_ref[3, 3] == 1
     gain = gain_ref[...]
 
-    def zero(i, _):
-        acc[i] = jnp.zeros((dim, 128), F32)
-        return 0
-
-    lax.fori_loop(0, places * 3, zero, 0)
-
     def one_block(b, parts):
         query_part, all_part = parts
         base = pl.multiple_of(b * SEGMENT, SEGMENT)
@@ -274,11 +284,7 @@
         wide = lax.div(count, WIDE)
         small = lax.div(lax.rem(count, WIDE), NARROW)
         rest = lax.rem(count, NARROW)
-        for h in range(per_group):
-            q = query_ref[pl.ds(base, SEGMENT), h * dim : (h + 1) * dim].astype(F32)
-            inverse = lax.rsqrt(jnp.mean(q * q, axis=-1, keepdims=True) + EPSILON)
-            qn[h * SEGMENT : (h + 1) * SEGMENT, :] = (q * inverse * gain).astype(BF16)
-        qt[...] = qn[...].astype(F32).T.astype(BF16)
+        qn, qt = qn_ref.at[b], qt_ref.at[b]
         m_ref[...] = jnp.full_like(m_ref, NEGATIVE)
         l_ref[...] = jnp.zeros_like(l_ref)
         o_ref[...] = jnp.zeros_like(o_ref)
@@ -286,9 +292,18 @@
         def starts(first, size):
             return [pl.multiple_of(list_ref[b, first + j], SEGMENT) for j in range(size)]
 
-        def first_starts():
-            ps = [0] + [jnp.where(j <= rest, j, 0) for j in range(1, NARROW)]
-            return [pl.multiple_of(list_ref[b, p], SEGMENT) for p in ps]
+        def first(step):
+            def at(size):
+                ps = [0] + [jnp.where(j <= rest, j, 0) for j in range(1, size)]
+                return [pl.multiple_of(list_ref[b, p], SEGMENT) for p in ps]
+
+            @pl.when(rest < SMALL)
+            def _():
+                step(0, at(SMALL))
+
+            @pl.when(rest >= SMALL)
+            def _():
+                step(0, at(NARROW))
 
         def tile(at, offset):
             return jnp.concatenate([kv_ref[pl.ds(s + offset, SEGMENT), :] for s in at], axis=0)
@@ -382,10 +397,10 @@
             lax.fori_loop(0, small, narrow, 0)
             lax.fori_loop(0, wide, broad, 0)
 
-        logits(0, first_starts(), True)
+        first(lambda slot, at: logits(slot, at, True))
         over(lambda slot, at: logits(slot, at, False))
         m_ref[...] = jnp.broadcast_to(jnp.max(m_ref[...], axis=-1, keepdims=True), m_ref.shape)
-        weights(0, first_starts())
+        first(weights)
         over(weights)
         total = jnp.sum(l_ref[...], axis=-1, keepdims=True)
         over_total = 1.0 / total
@@ -399,7 +414,7 @@
             delta = jnp.sum(g.astype(F32) * output[sl], axis=-1, keepdims=True)
             m_ref[sl, :] = jnp.broadcast_to(delta, (SEGMENT, 128))
         dot_t[...] = dop[...].astype(F32).T.astype(BF16)
-        slopes(0, first_starts())
+        first(slopes)
         over(slopes)
         raw = o_ref[...].T
         for h in range(per_group):
@@ -448,7 +463,7 @@
     gain_out[...] = jnp.where(row == 3, image_sum, filled)
 
 
-def attention(lists, query_input, output_grad, query_gain, kv):
+def attention(lists, query_input, output_grad, query_gain, kv, qn, qt, sums):
     rows, columns = query_input.shape
     per_group = columns // 128
     stacked = SEGMENT * per_group
@@ -462,18 +477,19 @@
             jax.ShapeDtypeStruct((rows, columns), BF16),
             VMEM((8, 128), F32),
             VMEM((kv.shape[0], 384, 128), BF16),
+            VMEM(sums.shape, F32),
         ),
-        in_specs=[pl.BlockSpec(memory_space=pltpu.SMEM)] + [whole] * 4,
-        out_specs=(whole,) * 3,
+        in_specs=[pl.BlockSpec(memory_space=pltpu.SMEM)] + [whole] * 7,
+        out_specs=(whole,) * 4,
+        input_output_aliases={7: 3},
         scratch_shapes=[
-            VMEM((stacked, 128), BF16), VMEM((128, stacked), BF16), VMEM((stacked, 128), BF16), VMEM((128, stacked), BF16),
+            VMEM((stacked, 128), BF16), VMEM((128, stacked), BF16),
             VMEM((slots, stacked, LANES), F32), VMEM((slots, stacked, LANES), BF16),
             VMEM((stacked, 128), F32), VMEM((stacked, 128), F32), VMEM((128, stacked), F32),
-            VMEM((segments, 128, 128), F32),
         ],
         compiler_params=pltpu.CompilerParams(vmem_limit_bytes=40 * MIB),
         name="attention",
-    )(lists, query_input, output_grad, query_gain, kv.reshape(flat, 128))
+    )(lists, query_input, output_grad, query_gain, kv.reshape(flat, 128), qn, qt, sums)
 
 
 def reduce_kernel(
@@ -641,11 +657,11 @@
 def shards(
     query_input, key_input, value_input, output_grad, query_gain, key_gain, stripe_order, frame_index, cross_blocks
 ):
-    kv, lists, queries, grads, gain = gathered(
+    kv, lists, queries, grads, gain, qn, qt, sums = gathered(
         key_input, value_input, key_gain, stripe_order[None], frame_index[None], cross_blocks,
         query_input, output_grad, query_gain,
     )
-    query_grad, gain_part, part = attention(lists, queries, grads, gain, kv)
+    query_grad, gain_part, part, _ = attention(lists, queries, grads, gain, kv, qn, qt, sums)
     key_grad, value_grad, gain_grads = reduced(part.reshape(kv.shape), gain_part, key_input, key_gain)
     return query_grad, key_grad, value_grad, gain_grads[:, None, :]
 

time: 71.7 us -> 70.4 us (0.982); the launches traced: 72.5 us -> 69 us
  Pallas kernels: 70 us -> 66.5 us
    pallas_call x1, Pallas kernels: 25.1 us -> 20.5 us  [reduced(): pl.pallas_call(reduce_kernel, out_shape=(VMEM((rows, dim), BF16), VMEM((r...]
    pallas_call x1, Pallas kernels: 23.6 us -> 24.8 us  [attention(): pl.pallas_call(functools.partial(attention_kernel, per_group, rows // SEG...]
where the time goes in v4:
time: 70.4 us; the launch traced here: 69 us
  Pallas kernels  66.5 us (94%)
  local copies, waits for them, and re-layouts  1.81 us (3%)
    pallas_call x1, Pallas kernels, attention(): pl.pallas_call(functools.partial(attention_kernel, per_group, rows // SEG...  24.8 us
    pallas_call x1, Pallas kernels, gathered(): pl.pallas_call(gather_kernel, out_shape=(VMEM((32, 2, rows, dim), BF16),...  21.3 us
    pallas_call x1, Pallas kernels, reduced(): pl.pallas_call(reduce_kernel, out_shape=(VMEM((rows, dim), BF16), VMEM((r...  20.5 us
    unnamed x7, local copies, waits for them, and re-layouts  1.81 us

profile of v4, /device:TPU:1, one launch (start us, length us, event | category | flops | bytes accessed | tf_op | source)
XLA Modules:
  0.0 69.0 jit_solution(16483148254308620897)
XLA Ops:
  0.6 0.0 copy-start.1
  0.6 21.3 %gather_keys.1 = (bf16[32,2,192,128]{3,2,1,0:T(8,128)(2,1)S(1)}, s32[8,128]{1,0:T(8,128)S(1)}, bf16[192,896]{1,0:T(8,128)(2,1)S(1)}, bf16[192,896]{1,0:T(8,128)(...) custom-call(bf16[192,128]{1,0:T(8,128)(2,1)} %key_hbm.3, ...), custom_call_target="tpu_custom_call" | custom-call | bytes 60000000 | tf_op jit(solution)/shard_map/gather_keys/pallas_call | solution.py:249
  21.9 0.0 copy-start
  21.9 24.8 %attention.1 = (bf16[192,896]{1,0:T(8,128)(2,1)}, f32[8,128]{1,0:T(8,128)S(1)}, bf16[32,384,128]{2,1,0:T(8,128)(2,1)S(1)}, f32[96,128,128]{2,1,0:T(8,128)S(1)}) custom-call(s32[8,128]{1,0:T(8,128)S(1)} %get-tuple-element.18.list_ref, bf16[192,896]{1,0:T(8,128)(2,1)S(1)} %get-tuple-element.19.query_ref, ...), custom_call_target="tpu_custom_call", output_to_operand_aliasing={{3}: (7, {})} | custom-call | tf_op jit(solution)/shard_map/attention/pallas_call | solution.py:474
  46.7 0.0 copy-done.1
  46.7 0.0 copy-done
  46.7 20.5 %reduce_keys.1 = (bf16[192,128]{1,0:T(8,128)(2,1)S(1)}, bf16[192,128]{1,0:T(8,128)(2,1)S(1)}, f32[2,128]{1,0:T(2,128)S(1)}) custom-call(bf16[32,2,192,128]{3,2,1,0:T(8,128)(2,1)S(1)} %bitcast.8, f32[8,128]{1,0:T(8,128)S(1)} %get-tuple-element.28.gain_part, bf16[192,128]{1,0:T(8,128)(2,1)S(1)} %copy-done, f32[1,128]{1,0:T(1,128)S(1)} %copy-done.1), custom_call_target="tpu_custom_call" | custom-call | tf_op jit(solution)/shard_map/reduce_keys/pallas_call | solution.py:636
  67.2 0.6 copy.19
  67.8 0.6 copy.21
  68.4 0.6 copy.20
Async XLA Ops:
  0.6 46.1 %copy-start.1 = (f32[1,128]{1,0:T(1,128)S(1)}, f32[1,128]{1,0:T(1,128)}, u32[]{:S(2)}) copy-start(f32[1,128]{1,0:T(1,128)} %gain_hbm.3) | copy-start | bytes 1540
  21.9 24.8 %copy-start = (bf16[192,128]{1,0:T(8,128)(2,1)S(1)}, bf16[192,128]{1,0:T(8,128)(2,1)}, u32[]{:S(2)}) copy-start(bf16[192,128]{1,0:T(8,128)(2,1)} %key_hbm.3) | copy-start | bytes 147460
